TPU v7x, 128 devices: a whole 4x4x4 slice. The times are simulated.
128 devices in a mesh: ctx: 16 (over z, x), kvh: 8 (over y, core).
Axes of the slice: x: 4, y: 4, z: 4, core: 2. Of those that a mesh axis runs over, the one named last changes fastest.
Arguments:
- queries: bfloat16 [16384, 8192], P('ctx', 'kvh'), may hold values from -8 to 8
- keys: bfloat16 [16384, 1024], P(('ctx', 'kvh')), may hold values from -8 to 8
- values: bfloat16 [16384, 1024], P(('ctx', 'kvh')), may hold values from -6 to 6
- out_grad: bfloat16 [16384, 8192], P('ctx', 'kvh'), may hold values from -6 to 6
- random_blocks: int32 [128, 3], replicated, may hold values from 8 to 127, as said below
Outputs:
- attended: bfloat16 [16384, 8192], P('ctx', 'kvh')
- query_grad: bfloat16 [16384, 8192], P('ctx', 'kvh')
- key_grad: bfloat16 [16384, 1024], P(('ctx', 'kvh'))
- value_grad: bfloat16 [16384, 1024], P(('ctx', 'kvh'))
Inputs may be any that keep to these rules, and one draw needn't show every extreme that they name: `random_blocks`: block b lies on ctx index b // 8. For each query block the 3 named blocks lie on 3 different ctx indices, none of them 0, the index holding the query block, or its two neighbours. Over the 8 rows of one ctx index, the named blocks (repeats counted) fall on 12 ctx indices as evenly as possible: none holds more than 2 of them and some holds exactly 2.
All inputs are finite; a program needn't handle non-finite values.
Results may differ from a plain program's by a relative error of at most 0.014.
Values may be sent and summed in bfloat16 or wider, within the bound.
A program may use at most 128 MiB of HBM per device.

v0:
```python
from functools import partial

import jax
import jax.numpy as jnp
from jax import lax
from jax.sharding import PartitionSpec as P

HD = 128
BLK = 128
GLOB = 2


def attend_block(operands, score_scale):
    query_rows, grad_rows, key_rows, value_rows, usable = operands
    scores = (
        jnp.einsum("bgqd,kgd->gqbk", query_rows, key_rows, preferred_element_type=jnp.float32)
        * score_scale
    )
    scores = jnp.where(usable, scores, -jnp.inf)
    largest = jnp.max(scores, axis=-1, keepdims=True)
    raised = jnp.exp(scores - largest)
    probs = raised / jnp.sum(raised, axis=-1, keepdims=True)
    weights = probs.astype(jnp.bfloat16)
    attended = jnp.einsum("gqbk,kgd->bgqd", weights, value_rows, preferred_element_type=jnp.float32)
    prob_grad = jnp.einsum(
        "bgqd,kgd->gqbk", grad_rows, value_rows, preferred_element_type=jnp.float32
    )
    centre = jnp.sum(probs * prob_grad, axis=-1, keepdims=True)
    score_grad = (probs * (prob_grad - centre) * score_scale).astype(jnp.bfloat16)
    query_grad = jnp.einsum(
        "gqbk,kgd->bgqd", score_grad, key_rows, preferred_element_type=jnp.float32
    )
    key_grad = jnp.einsum(
        "gqbk,bgqd->kgd", score_grad, query_rows, preferred_element_type=jnp.float32
    )
    value_grad = jnp.einsum(
        "gqbk,bgqd->kgd", weights, grad_rows, preferred_element_type=jnp.float32
    )
    return (attended.astype(jnp.bfloat16), query_grad.astype(jnp.bfloat16), key_grad, value_grad)


def per_device(queries, keys, values, out_grad, random_blocks):
    block_len = BLK
    ctx_count = lax.axis_size("ctx")
    ctx_index = lax.axis_index("ctx")
    stacked = jnp.stack([keys, values])
    local_kv = lax.all_to_all(stacked, "kvh", split_axis=2, concat_axis=1, tiled=True)
    tok_rows = local_kv.shape[1]
    row_width = local_kv.shape[2]
    groups = row_width // HD
    query_blocks = tok_rows // block_len
    all_blocks = query_blocks * ctx_count
    rand_count = random_blocks.shape[1]
    select_count = 3 + GLOB + rand_count
    first_block = ctx_index * query_blocks
    my_random = lax.dynamic_slice_in_dim(random_blocks, first_block, query_blocks, 0)
    block_ids = first_block + jnp.arange(query_blocks, dtype=jnp.int32)
    window_ids = block_ids[:, None] - 1 + jnp.arange(3, dtype=jnp.int32)[None, :]
    window_ok = (window_ids >= GLOB) & (window_ids < all_blocks)
    entry_ok = jnp.concatenate(
        [window_ok, jnp.ones((query_blocks, GLOB + rand_count), jnp.bool_)], axis=1
    )
    usable = jnp.repeat(entry_ok, block_len, axis=1)
    whole_kv = lax.all_gather(local_kv, "ctx", axis=1, tiled=True)
    whole_blocks = whole_kv.reshape(2, all_blocks, block_len, row_width)
    global_ids = jnp.broadcast_to(jnp.arange(GLOB, dtype=jnp.int32)[None, :], (query_blocks, GLOB))
    listed = jnp.concatenate([window_ids, global_ids, my_random], axis=1)
    listed = jnp.clip(listed, 0, all_blocks - 1)
    selected = whole_blocks[:, listed]
    query_rows = queries.reshape(query_blocks, block_len, groups, -1, HD)
    grad_rows = out_grad.reshape(query_blocks, block_len, groups, -1, HD)
    key_chosen = selected[0].reshape(query_blocks, select_count * block_len, groups, HD)
    value_chosen = selected[1].reshape(query_blocks, select_count * block_len, groups, HD)
    attended, query_grad, key_part, value_part = lax.map(
        partial(attend_block, score_scale=HD ** (-0.5)),
        (query_rows, grad_rows, key_chosen, value_chosen, usable),
    )
    grad_parts = jnp.stack([key_part, value_part]).reshape(
        2, query_blocks, select_count, block_len, row_width
    )
    listed_flat = listed.reshape(-1)
    entry_flat = entry_ok.reshape(-1)
    part_flat = grad_parts.reshape(2, query_blocks * select_count, block_len, row_width)
    kept_parts = jnp.where(entry_flat[None, :, None, None], part_flat, 0.0)
    placed = (
        jnp.zeros((2, all_blocks, block_len, row_width), jnp.float32)
        .at[:, listed_flat]
        .add(kept_parts)
    )
    placed_rows = jnp.moveaxis(placed, 0, 2).reshape(all_blocks * block_len, 2 * row_width)
    shares = lax.psum_scatter(
        placed_rows.astype(jnp.bfloat16), "ctx", scatter_dimension=0, tiled=True
    ).astype(jnp.float32)
    total_grad = jnp.moveaxis(shares.reshape(tok_rows, 2, row_width), 1, 0)
    rounded = total_grad.astype(jnp.bfloat16)
    home_grads = lax.all_to_all(rounded, "kvh", split_axis=1, concat_axis=2, tiled=True)
    return (
        attended.reshape(tok_rows, -1),
        query_grad.reshape(tok_rows, -1),
        home_grads[0],
        home_grads[1],
    )


def solution(mesh):
    in_specs = (
        P("ctx", "kvh"),
        P(("ctx", "kvh"), None),
        P(("ctx", "kvh"), None),
        P("ctx", "kvh"),
        P(),
    )
    out_specs = (P("ctx", "kvh"), P("ctx", "kvh"), P(("ctx", "kvh"), None), P(("ctx", "kvh"), None))
    return jax.shard_map(
        per_device, mesh=mesh, in_specs=in_specs, out_specs=out_specs, check_vma=False
    )
```

profile of v0, /device:TPU:1, one launch (start us, length us, event | category | flops | bytes accessed | tf_op | source)
XLA Modules:
  0.0 476.6 jit_solution(15260468992121076992)
XLA Ops:
  8.9 15.1 %all_to_all.33 = bf16[2,128,1024]{1,0,2:T(2,128)(2,1)S(1)} all-to-all(bf16[2,128,1024]{1,0,2:T(2,128)(2,1)S(1)} %copy.108), channel_id=1, replica_groups=mesh['ctx'=16,'kvh'=8] {'kvh'}, dimensions={2} | all-to-all | bytes 1048576 | tf_op jit(solution)/shard_map/all_to_all | solution.py:47
  25.8 1.9 copy.151
  27.8 2.0 copy.152
  29.8 66.9 %all-gather.2.cloned.1.call-done = bf16[2,16384,128]{2,1,0:T(8,128)(2,1)} async-done(((bf16[2,1024,128]{2,1,0:T(8,128)(2,1)}), bf16[2,16384,128]{2,1,0:T(8,128)(2,1)}) %all-gather.2.cloned.1.call-update) | async-done | bytes 8388624 | tf_op jit(solution)/shard_map/all_gather | solution.py:64
  96.7 6.4 %gather_fusion = bf16[64,2,128,128]{3,2,1,0:T(8,128)(2,1)} fusion(bf16[2,128,128,128]{3,2,1,0:T(8,128)(2,1)} %bitcast.272, s32[1024]{0:T(1024)S(1)} %pad_clamp_fusion), kind=kCustom, calls=%fused_computation | custom fusion | bytes 8388864 | tf_op jit(solution)/shard_map/gather | solution.py:69
  103.1 4.8 %fusion.45 = (bf16[1,8,8,128,128]{4,3,0,2,1:T(8,128)(2,1)}, bf16[1,8,8,128,128]{4,3,0,2,1:T(8,128)(2,1)}) fusion(bf16[2,8,8,128,128]{4,3,0,2,1:T(8,128)(2,1)} %bitcast.258), kind=kLoop, calls=%fused_computation.70 | loop fusion | bytes 8388608 | tf_op jit(solution)/shard_map/slice | solution.py:72
  107.9 177.8 %while.16 = (s32[]{:T(128)}, bf16[8,128,1,8,128]{4,3,1,0,2:T(8,128)(2,1)}, bf16[8,128,1,8,128]{4,3,1,0,2:T(8,128)(2,1)}, f32[8,1024,1,128]{3,1,0,2:T(8,128)}, f3...) while((s32[]{:T(128)}, ...), condition=%wide.region_4.5_spmd, body=%wide.region_0.4_spmd.sunk | while | flops 1643377664 | bytes 84472016 | solution.py:74
  109.9 1.7 bitcast_reduce_fusion.2
  113.5 2.3 fusion.71
  116.1 3.6 fusion.72
  119.9 3.8 fusion.68
  123.7 1.9 fusion.69
  126.5 1.4 fusion.70
  132.2 1.7 bitcast_reduce_fusion.2
  135.8 2.3 fusion.71
  138.3 3.6 fusion.72
  142.1 3.8 fusion.68
  146.0 1.9 fusion.69
  148.7 1.4 fusion.70
  154.4 1.7 bitcast_reduce_fusion.2
  158.1 2.3 fusion.71
  160.6 3.6 fusion.72
  164.4 3.8 fusion.68
  168.2 1.9 fusion.69
  171.0 1.4 fusion.70
  176.6 1.7 bitcast_reduce_fusion.2
  180.3 2.3 fusion.71
  182.8 3.6 fusion.72
  186.6 3.8 fusion.68
  190.4 1.9 fusion.69
  198.8 1.7 bitcast_reduce_fusion.2
  202.5 2.3 fusion.71
  205.0 3.6 fusion.72
  208.8 3.8 fusion.68
  212.6 1.9 fusion.69
  221.1 1.7 bitcast_reduce_fusion.2
  224.7 2.3 fusion.71
  227.2 3.6 fusion.72
  231.0 3.8 fusion.68
  234.8 1.9 fusion.69
  243.3 1.7 bitcast_reduce_fusion.2
  246.9 2.3 fusion.71
  249.4 3.6 fusion.72
  253.2 3.8 fusion.68
  257.0 1.9 fusion.69
  265.5 1.7 bitcast_reduce_fusion.2
  269.1 2.3 fusion.71
  271.6 3.6 fusion.72
  275.4 3.8 fusion.68
  279.2 1.9 fusion.69
  282.0 1.4 fusion.70
  285.7 4.0 fusion.39
  289.7 3.8 copy.121
  293.5 7.9 %broadcast_in_dim.60 = f32[2,128,128,128]{3,2,1,0:T(8,128)} broadcast(f32[]{:T(128)} %constant.13.clone.1), dimensions={} | broadcast | bytes 16777220 | tf_op jit(solution)/shard_map/broadcast_in_dim | solution.py:86
  301.4 19.1 %scatter_fusion = f32[2,128,128,128]{3,2,1,0:T(8,128)} fusion(f32[2,128,128,128]{3,2,1,0:T(8,128)} %broadcast_in_dim.60, s32[64]{0:T(128)S(1)} %fusion.44, f32[64,2,128,128]{3,2,1,0:T(8,128)} %copy.121), kind=kCustom, calls=%fused_computation.1 | custom fusion | flops 2097152 | bytes 25166080 | tf_op jit(solution)/shard_map/scatter-add | solution.py:88
  320.5 9.2 %convert_bitcast_fusion = bf16[128,128,2,128]{3,1,0,2:T(8,128)(2,1)} fusion(f32[2,128,128,128]{3,2,1,0:T(8,128)} %scatter_fusion), kind=kLoop, calls=%fused_computation.52 | loop fusion | flops 4194304 | bytes 25165824 | tf_op jit(solution)/shard_map/convert_element_type | solution.py:92
  329.7 12.4 %copy.122 = bf16[128,128,2,128]{1,0,3,2:T(8,128)(2,1)} copy(bf16[128,128,2,128]{3,1,0,2:T(8,128)(2,1)} %convert_bitcast_fusion) | data formatting | bytes 16777216 | tf_op jit(solution)/shard_map/convert_element_type | solution.py:92
  342.1 23.2 %copy.169 = bf16[32,8,128,128]{3,1,2,0:T(8,128)(2,1)} copy(bf16[32,8,128,128]{3,2,1,0:T(8,128)(2,1)} %bitcast.257) | data formatting | bytes 16777216
  365.4 84.4 %reduce-scatter.2.cloned.1.call-done = bf16[1024,256]{0,1:T(8,128)(2,1)} async-done(((bf16[16384,256]{0,1:T(8,128)(2,1)}), bf16[1024,256]{0,1:T(8,128)(2,1)}) %reduce-scatter.2.cloned.1.call-update) | async-done | bytes 524304 | tf_op jit(solution)/shard_map/reduce_scatter | solution.py:91
  449.8 2.0 copy.123
  451.8 6.4 %all-to-all-start.1 = ((bf16[2,1024,128]{2,0,1:T(2,128)(2,1)}), bf16[2,1024,128]{2,0,1:T(2,128)(2,1)S(1)}, u32[]{:S(2)}, u32[]{:S(2)}) async-start(bf16[2,1024,128]{2,0,1:T(2,128)(2,1)} %bitcast.49), calls=%async_computation.2 | async-start | bytes 1048576 | tf_op jit(solution)/shard_map/all_to_all | solution.py:96
  458.2 3.5 copy.171
  461.7 1.9 copy.170
  463.7 3.9 all-to-all-done.1
  (167 shorter events, 70.2 us)
Async XLA Ops:
  7.2 18.2 %copy-start.5 = (s32[128,3]{0,1:T(4,128)S(1)}, s32[128,3]{0,1:T(4,128)}, u32[]{:S(2)}) copy-start(s32[128,3]{0,1:T(4,128)} %param.11) | copy-start | bytes 4612
  7.2 18.6 %copy-start.2 = (bf16[1024,1024]{1,0:T(8,128)(2,1)S(1)}, bf16[1024,1024]{1,0:T(8,128)(2,1)}, u32[]{:S(2)}) copy-start(bf16[1024,1024]{1,0:T(8,128)(2,1)} %param.7) | copy-start | bytes 6291460
  7.2 89.5 %all-gather.2.cloned.1.call-start = ((), (), s32[]{:S(2)}) async-start(), calls=%async_computation.3 | async-start | bytes 8912896 | tf_op jit(solution)/shard_map/all_gather | solution.py:64
  25.1 424.7 %reduce-scatter.2.cloned.1.call-start = ((), (), s32[]{:S(2)}) async-start(), calls=%async_computation.4 | async-start | bytes 8912896 | tf_op jit(solution)/shard_map/reduce_scatter | solution.py:91
  25.8 2.0 copy-start.3
  111.6 1.9 copy-start
  119.9 3.8 copy-start.1
  133.9 1.9 copy-start
  142.1 3.8 copy-start.1
  156.1 1.9 copy-start
  164.4 3.8 copy-start.1
  178.3 1.9 copy-start
  186.6 3.8 copy-start.1
  200.5 1.9 copy-start
  208.8 3.8 copy-start.1
  222.8 1.9 copy-start
  231.0 3.8 copy-start.1
  245.0 1.9 copy-start
  253.2 3.8 copy-start.1
  267.2 1.9 copy-start
  275.4 3.8 copy-start.1
  365.4 96.4 %copy-start.4 = (bf16[8,128,1,8,128]{4,3,1,0,2:T(8,128)(2,1)S(1)}, bf16[8,128,1,8,128]{4,3,1,0,2:T(8,128)(2,1)}, u32[]{:S(2)}) copy-start(bf16[8,128,1,8,128]{4,3,1,0,2:T(8,128)(2,1)} %get-tuple-element.60) | copy-start | bytes 6291460
  451.8 15.7 %all-to-all-start.1 = ((bf16[2,1024,128]{2,0,1:T(2,128)(2,1)}), bf16[2,1024,128]{2,0,1:T(2,128)(2,1)S(1)}, u32[]{:S(2)}, u32[]{:S(2)}) async-start(bf16[2,1024,128]{2,0,1:T(2,128)(2,1)} %bitcast.49), calls=%async_computation.2 | async-start | bytes 1048576 | tf_op jit(solution)/shard_map/all_to_all | solution.py:96
Sparse Core Ops, SparseCore 0:
  25.2 71.4 all-gather.1
  365.5 84.2 reduce-scatter.1
where the time goes:
time: 479 us; the launch traced here: 477 us
  waiting for transfers between devices  155 us (32%)
  local copies, waits for them, and re-layouts  119 us (25%)
  matrix products  109 us (23%)
  other arithmetic  56.6 us (12%)
  blocking collectives  15.1 us (3%)
  between operations  14.2 us (3%)
  starting transfers between devices  6.46 us (1%)
    reduce_scatter x1, waiting for transfers between devices, per_device(): lax.psum_scatter(placed_rows.astype(jnp.bfloat16), 'ctx', scatter_dimensi...  84.4 us
    all_gather x1, waiting for transfers between devices, per_device(): whole_kv = lax.all_gather(local_kv, 'ctx', axis=1, tiled=True)  66.9 us
    unnamed x15, local copies, waits for them, and re-layouts  34.3 us
    dot_general x8, matrix products, attend_block(): jnp.einsum('bgqd,kgd->gqbk', grad_rows, value_rows, preferred_element_typ...  30.4 us
    dot_general x8, matrix products, attend_block(): jnp.einsum('gqbk,bgqd->kgd', weights, grad_rows, preferred_element_type=j...  28.8 us
    dynamic_update_slice x48, local copies, waits for them, and re-layouts, per_device(): lax.map(partial(attend_block, score_scale=HD ** (-0.5)), (query_rows, gra...  21 us
    scatter-add x1, other arithmetic, per_device(): placed = jnp.zeros((2, all_blocks, block_len, row_width), jnp.float32).at...  19.1 us
    dot_general x8, matrix products, attend_block(): jnp.einsum('gqbk,kgd->bgqd', weights, value_rows, preferred_element_type=...  18.4 us
  transfers between devices with their start and end apart: 3, of which 3 were waited for; matrix products, arithmetic and copies ran while one was open for 2% of the time, Pallas kernels for 0%

commit v1 on v0

v1 whole, which is shorter than its diff:
```python
import functools

import jax
import jax.numpy as jnp
from jax import lax
from jax.experimental import pallas as pl
from jax.experimental.pallas import tpu as pltpu
from jax.sharding import PartitionSpec as P

HD = 128
BLK = 128
GLOB = 2
RAND = 3
QB = 8
CTX = 16
KVH = 8
HEADS = 8
SLOTS = 2
NKB = QB * CTX
EXTRA = QB
RECV = QB + 1
POOL = RECV + CTX * SLOTS
ENTRIES = 3 + GLOB + RAND
CHUNK = 512
SCALE = HD**-0.5
LOG2E = 1.4426950408889634
MASKED = -1e30

NT = (((1,), (1,)), ((), ()))
TN = (((0,), (0,)), ((), ()))


def mm(a, b, dims=(((1,), (0,)), ((), ()))):
    return lax.dot_general(a, b, dims, preferred_element_type=jnp.float32)


def slot_blocks(rand, me, dest):
    first = jnp.int32(0)
    second = jnp.int32(0)
    count = jnp.int32(0)
    for e in range(QB * RAND):
        r = rand[dest * (QB * RAND) + e]
        hit = (r // QB) == me
        local = r % QB
        first = jnp.where(hit & (count == 0), local, first)
        second = jnp.where(hit & (count == 1), local, second)
        count = count + hit.astype(jnp.int32)
    first = jnp.where(dest == me + 1, QB - 1, first)
    first = jnp.where(me == 0, 0, first)
    second = jnp.where(me == 0, 1, second)
    return first, second


def pack_kernel(rand, kv_ref, out_ref):
    me = lax.axis_index("ctx")

    def body(dest, carry):
        for k, local in enumerate(slot_blocks(rand, me, dest)):
            for t in range(2):
                out_ref[dest, k, t] = kv_ref[t, local]
        return carry

    lax.fori_loop(0, CTX, body, 0)


def attend_kernel(
    rand, q_ref, g_ref, kv_ref, recv_ref, extra_ref,
    o_ref, dq_ref, local_ref, back_ref, back_extra_ref,
    pool, grads, kall, vall, dk, dv, table, fill,
):
    me = lax.axis_index("ctx")
    i = pl.program_id(0)

    @pl.when(i == 0)
    def _():
        for t in range(2):
            for b in range(QB):
                pool[b, t] = kv_ref[t, b]
            pool[EXTRA, t] = extra_ref[t]
        for s in range(CTX):
            for k in range(SLOTS):
                for t in range(2):
                    pool[RECV + s * SLOTS + k, t] = recv_ref[s, k, t]
        grads[...] = jnp.zeros_like(grads)
        for s in range(CTX):
            fill[s] = 0

    for e in range(3):
        gid = me * QB + i - 1 + e
        near = i - 1 + e
        before = jnp.where(me == 1, EXTRA, RECV + (me - 1) * SLOTS)
        after = RECV + (me + 1) * SLOTS
        place = jnp.where(near < 0, before, jnp.where(near >= QB, after, near))
        ok = (gid >= GLOB) & (gid < NKB)
        table[e] = jnp.where(ok, place, 0)
    for e in range(GLOB):
        table[3 + e] = jnp.where(me == 0, e, RECV + e)
    for e in range(RAND):
        r = rand[(me * QB + i) * RAND + e]
        owner = r // QB
        rank = fill[owner]
        fill[owner] = rank + 1
        table[3 + GLOB + e] = RECV + owner * SLOTS + rank

    for e in range(ENTRIES):
        kall[e * BLK : (e + 1) * BLK, :] = pool[table[e], 0]
        vall[e * BLK : (e + 1) * BLK, :] = pool[table[e], 1]
    dk[...] = jnp.zeros_like(dk)
    dv[...] = jnp.zeros_like(dv)
    per = CHUNK // BLK

    def chunk(j, carry):
        cols = [pl.ds(pl.multiple_of((j * per + t) * HD, HD), HD) for t in range(per)]
        q = jnp.concatenate([q_ref[:, c] for c in cols], 0)
        g = jnp.concatenate([g_ref[:, c] for c in cols], 0)
        s = mm(q, kall[...], NT)
        parts = []
        for e in range(ENTRIES):
            part = s[:, e * BLK : (e + 1) * BLK]
            if e < 3:
                gid = me * QB + i - 1 + e
                ok = (gid >= GLOB) & (gid < NKB)
                part = part + jnp.where(ok, 0.0, MASKED).astype(jnp.float32)
            parts.append(part)
        s = jnp.concatenate(parts, 1)
        top = jnp.max(s, 1, keepdims=True)
        p = jnp.exp2(s * (SCALE * LOG2E) - top * (SCALE * LOG2E))
        inv = 1.0 / jnp.sum(p, 1, keepdims=True)
        pb = p.astype(jnp.bfloat16)
        o = mm(pb, vall[...]) * inv
        gb = (g.astype(jnp.float32) * inv).astype(jnp.bfloat16)
        centre = jnp.sum(gb.astype(jnp.float32) * o, 1, keepdims=True)
        dp = mm(gb, vall[...], NT)
        ds = (p * (dp - centre)).astype(jnp.bfloat16)
        dq = mm(ds, kall[...]) * SCALE
        for t in range(per):
            rows = slice(t * BLK, (t + 1) * BLK)
            o_ref[:, cols[t]] = o[rows].astype(jnp.bfloat16)
            dq_ref[:, cols[t]] = dq[rows].astype(jnp.bfloat16)
        dv[...] += mm(gb, pb, TN)
        dk[...] += mm(q, ds, TN)
        return carry

    lax.fori_loop(0, HEADS * BLK // CHUNK, chunk, 0)
    for e in range(ENTRIES):
        cols = slice(e * BLK, (e + 1) * BLK)
        grads[table[e], 0] = grads[table[e], 0] + dk[:, cols] * SCALE
        grads[table[e], 1] = grads[table[e], 1] + dv[:, cols]

    @pl.when(i == QB - 1)
    def _():
        for t in range(2):
            for b in range(QB):
                local_ref[b, t] = grads[b, t]
            back_extra_ref[t] = grads[EXTRA, t].astype(jnp.bfloat16)
        for s in range(CTX):
            for k in range(SLOTS):
                for t in range(2):
                    back_ref[s, k, t] = grads[RECV + s * SLOTS + k, t].astype(jnp.bfloat16)


def total_kernel(rand, local_ref, back_ref, extra_ref, out_ref, acc):
    me = lax.axis_index("ctx")
    acc[...] = local_ref[...]

    def body(src, carry):
        for k, local in enumerate(slot_blocks(rand, me, src)):
            for t in range(2):
                acc[local, t] = acc[local, t] + back_ref[src, k, t].astype(jnp.float32)
        return carry

    lax.fori_loop(0, CTX, body, 0)
    for t in range(2):
        acc[QB - 1, t] = acc[QB - 1, t] + extra_ref[t].astype(jnp.float32)
    for t in range(2):
        for b in range(QB):
            out_ref[t, b] = acc[b, t].T.astype(jnp.bfloat16)


VM = pl.BlockSpec(memory_space=pltpu.VMEM)
SM = pl.BlockSpec(memory_space=pltpu.SMEM)
BIG = pltpu.CompilerParams(vmem_limit_bytes=56 * 2**20)


def per_device(queries, keys, values, out_grad, random_blocks):
    rand = random_blocks.reshape(-1)
    bf = jnp.bfloat16
    stacked = jnp.stack([keys, values])
    kv = lax.all_to_all(stacked, "kvh", split_axis=2, concat_axis=1, tiled=True)
    kv = kv.reshape(2, QB, BLK, HD)
    extra = lax.ppermute(kv[:, QB - 1], "ctx", [(0, 1)])
    send = pl.pallas_call(
        pack_kernel,
        out_shape=jax.ShapeDtypeStruct((CTX, SLOTS, 2, BLK, HD), bf),
        in_specs=[SM, VM],
        out_specs=VM,
        compiler_params=BIG,
    )(rand, kv)
    recv = lax.all_to_all(send, "ctx", split_axis=0, concat_axis=0, tiled=True)
    whole = lambda shape: pl.BlockSpec(shape, lambda i, *_: (0,) * len(shape))
    rows = pl.BlockSpec((BLK, HEADS * HD), lambda i, *_: (i, 0))
    tok = QB * BLK
    attended, query_grad, local, back, back_extra = pl.pallas_call(
        attend_kernel,
        grid_spec=pltpu.PrefetchScalarGridSpec(
            num_scalar_prefetch=1,
            grid=(QB,),
            in_specs=[
                rows,
                rows,
                whole((2, QB, BLK, HD)),
                whole((CTX, SLOTS, 2, BLK, HD)),
                whole((2, BLK, HD)),
            ],
            out_specs=[
                rows,
                rows,
                whole((QB, 2, HD, BLK)),
                whole((CTX, SLOTS, 2, HD, BLK)),
                whole((2, HD, BLK)),
            ],
            scratch_shapes=[
                pltpu.VMEM((POOL, 2, BLK, HD), bf),
                pltpu.VMEM((POOL, 2, HD, BLK), jnp.float32),
                pltpu.VMEM((ENTRIES * BLK, HD), bf),
                pltpu.VMEM((ENTRIES * BLK, HD), bf),
                pltpu.VMEM((HD, ENTRIES * BLK), jnp.float32),
                pltpu.VMEM((HD, ENTRIES * BLK), jnp.float32),
                pltpu.SMEM((ENTRIES,), jnp.int32),
                pltpu.SMEM((CTX,), jnp.int32),
            ],
        ),
        out_shape=[
            jax.ShapeDtypeStruct((tok, HEADS * HD), bf),
            jax.ShapeDtypeStruct((tok, HEADS * HD), bf),
            jax.ShapeDtypeStruct((QB, 2, HD, BLK), jnp.float32),
            jax.ShapeDtypeStruct((CTX, SLOTS, 2, HD, BLK), bf),
            jax.ShapeDtypeStruct((2, HD, BLK), bf),
        ],
        compiler_params=BIG,
    )(rand, queries, out_grad, kv, recv, extra)
    back = lax.all_to_all(back, "ctx", split_axis=0, concat_axis=0, tiled=True)
    back_extra = lax.ppermute(back_extra, "ctx", [(1, 0)])
    total = pl.pallas_call(
        total_kernel,
        out_shape=jax.ShapeDtypeStruct((2, QB, BLK, HD), bf),
        in_specs=[SM, VM, VM, VM],
        out_specs=VM,
        scratch_shapes=[pltpu.VMEM((QB, 2, HD, BLK), jnp.float32)],
        compiler_params=BIG,
    )(rand, local, back, back_extra)
    home = lax.all_to_all(
        total.reshape(2, tok, HD), "kvh", split_axis=1, concat_axis=2, tiled=True
    )
    return attended, query_grad, home[0], home[1]


def solution(mesh):
    in_specs = (
        P("ctx", "kvh"),
        P(("ctx", "kvh"), None),
        P(("ctx", "kvh"), None),
        P("ctx", "kvh"),
        P(),
    )
    out_specs = (P("ctx", "kvh"), P("ctx", "kvh"), P(("ctx", "kvh"), None), P(("ctx", "kvh"), None))
    return jax.shard_map(
        per_device, mesh=mesh, in_specs=in_specs, out_specs=out_specs, check_vma=False
    )
```

time: 479 us -> 165 us (0.34)
  matrix products: 109 us -> 0 us
  local copies, waits for them, and re-layouts: 119 us -> 10.2 us
  waiting for transfers between devices: 155 us -> 62.5 us
  other arithmetic: 56.6 us -> 1.08 us
  Pallas kernels: 0 us -> 52.4 us
  starting transfers between devices: 6.46 us -> 22.8 us
  between operations: 14.2 us -> 0.75 us
    dot_general x48 -> x0, matrix products: 109 us -> none  [the longest x8 30.4 us: attend_block(): jnp.einsum('bgqd,kgd->gqbk', grad_rows, value_rows, preferred_element_typ...]
    reduce_scatter x1 -> x0, waiting for transfers between devices: 84.4 us -> none  [per_device(): lax.psum_scatter(placed_rows.astype(jnp.bfloat16), 'ctx', scatter_dimensi...]
    all_gather x1 -> x0, waiting for transfers between devices: 66.9 us -> none  [per_device(): whole_kv = lax.all_gather(local_kv, 'ctx', axis=1, tiled=True)]
    pallas_call x0 -> x3, Pallas kernels: none -> 52.4 us  [the longest x1 40.1 us: per_device(): pl.pallas_call(attend_kernel, grid_spec=pltpu.PrefetchScalarGridSpec(num_...]
    ppermute x0 -> x2, waiting for transfers between devices: none -> 48.5 us  [the longest x1 26.1 us: per_device(): back_extra = lax.ppermute(back_extra, 'ctx', [(1, 0)])]
    unnamed x15 -> x13, local copies, waits for them, and re-layouts: 34.3 us -> 2.79 us
    dynamic_update_slice x48 -> x0, local copies, waits for them, and re-layouts: 21 us -> none  [per_device(): lax.map(partial(attend_block, score_scale=HD ** (-0.5)), (query_rows, gra...]
    scatter-add x1 -> x0, other arithmetic: 19.1 us -> none  [per_device(): placed = jnp.zeros((2, all_blocks, block_len, row_width), jnp.float32).at...]
  transfers between devices with their start and end apart: 3 -> 5, of which waited for: 3 -> 5; matrix products, arithmetic and copies ran while one was open for 2% -> 1% of each run, Pallas kernels for 0% -> 0%
where the time goes in v1:
time: 165 us; the launch traced here: 164 us
  waiting for transfers between devices  62.5 us (38%)
  Pallas kernels  52.4 us (32%)
  starting transfers between devices  22.8 us (14%)
  blocking collectives  14.4 us (9%)
  local copies, waits for them, and re-layouts  10.2 us (6%)
    pallas_call x1, Pallas kernels, per_device(): pl.pallas_call(attend_kernel, grid_spec=pltpu.PrefetchScalarGridSpec(num_...  40.1 us
    ppermute x1, waiting for transfers between devices, per_device(): back_extra = lax.ppermute(back_extra, 'ctx', [(1, 0)])  26.1 us
    ppermute x1, waiting for transfers between devices, per_device(): extra = lax.ppermute(kv[:, QB - 1], 'ctx', [(0, 1)])  22.4 us
    all_to_all x1, blocking collectives, per_device(): lax.all_to_all(total.reshape(2, tok, HD), 'kvh', split_axis=1, concat_axi...  14.4 us
    all_to_all x1, waiting for transfers between devices, per_device(): kv = lax.all_to_all(stacked, 'kvh', split_axis=2, concat_axis=1, tiled=True)  8.45 us
    all_to_all x1, starting transfers between devices, per_device(): recv = lax.all_to_all(send, 'ctx', split_axis=0, concat_axis=0, tiled=True)  7.6 us
    pallas_call x1, Pallas kernels, per_device(): pl.pallas_call(total_kernel, out_shape=jax.ShapeDtypeStruct((2, QB, BLK,...  6.52 us
    all_to_all x1, starting transfers between devices, per_device(): kv = lax.all_to_all(stacked, 'kvh', split_axis=2, concat_axis=1, tiled=True)  5.96 us
  transfers between devices with their start and end apart: 5, of which 5 were waited for; matrix products, arithmetic and copies ran while one was open for 1% of the time, Pallas kernels for 0%

profile of v1, /device:TPU:1, one launch (start us, length us, event | category | flops | bytes accessed | tf_op | source)
XLA Modules:
  0.0 164.2 jit_solution(16758096632134111764)
XLA Ops:
  0.6 0.0 copy-start.4
  0.6 1.1 pad_maximum_fusion
  1.7 1.1 copy.30
  2.8 6.0 %all-to-all-start = ((bf16[2,128,1024]{1,0,2:T(2,128)(2,1)}), bf16[2,128,1024]{1,0,2:T(2,128)(2,1)S(1)}, u32[]{:S(2)}, u32[]{:S(2)}) async-start(bf16[2,128,1024]{1,0,2:T(2,128)(2,1)} %copy.30), calls=%async_computation | async-start | bytes 1048576 | tf_op jit(solution)/shard_map/all_to_all | solution.py:189
  8.8 0.0 copy-done.4
  8.8 0.1 copy.29
  8.9 0.8 reshape.20.rand
  9.7 8.4 %all-to-all-done = bf16[2,128,1024]{1,0,2:T(2,128)(2,1)S(1)} async-done(((bf16[2,128,1024]{1,0,2:T(2,128)(2,1)}), bf16[2,128,1024]{1,0,2:T(2,128)(2,1)S(1)}, u32[]{:S(2)}, u32[]{:S(2)}) %all-to-all-start) | async-done | bytes 524320 | tf_op jit(solution)/shard_map/all_to_all | solution.py:189
  18.1 1.1 copy.40
  19.3 5.8 %shard_map.84 = bf16[16,2,2,128,128]{4,3,2,1,0:T(8,128)(2,1)} custom-call(s32[384]{0:T(512)} %reshape.20.rand, bf16[2,8,128,128]{3,2,1,0:T(8,128)(2,1)} %bitcast.19), custom_call_target="tpu_custom_call" | custom-call | tf_op jit(solution)/shard_map/pallas_call | solution.py:192
  25.0 7.6 %all-to-all-start.1 = ((bf16[16,2,2,128,128]{4,3,2,1,0:T(8,128)(2,1)}), bf16[16,2,2,128,128]{4,3,2,1,0:T(8,128)(2,1)S(1)}, u32[]{:S(2)}, u32[]{:S(2)}) async-start(bf16[16,2,2,128,128]{4,3,2,1,0:T(8,128)(2,1)} %shard_map.84), calls=%async_computation.1 | async-start | bytes 4194304 | tf_op jit(solution)/shard_map/all_to_all | solution.py:199
  32.6 0.4 copy.32
  33.1 3.3 %collective-permute-start = (bf16[2,128,128]{2,1,0:T(8,128)(2,1)S(1)}, bf16[2,128,128]{2,1,0:T(8,128)(2,1)S(1)}, u32[]{:S(2)}, u32[]{:S(2)}) collective-permute-start(bf16[2,128,128]{2,1,0:T(8,128)(2,1)S(1)} %slice_bitcast_fusion), channel_id=1, source_target_pairs={{0,8},{1,9},{2,10},{3,11},{4,12},{5,13},{6,14},{7,15}} | collective-permute-start | bytes 196616 | tf_op jit(solution)/shard_map/ppermute | solution.py:191
  36.4 22.4 %collective-permute-done.extra_ref = bf16[2,128,128]{2,1,0:T(8,128)(2,1)S(1)} collective-permute-done((bf16[2,128,128]{2,1,0:T(8,128)(2,1)S(1)}, bf16[2,128,128]{2,1,0:T(8,128)(2,1)S(1)}, u32[]{:S(2)}, u32[]{:S(2)}) %collective-permute-start) | collective-permute-done | bytes 65568 | tf_op jit(solution)/shard_map/ppermute | solution.py:191
  58.8 0.0 copy-start.2
  58.8 3.8 %all-to-all-done.1.recv_ref = bf16[16,2,2,128,128]{4,3,2,1,0:T(8,128)(2,1)S(1)} async-done(((bf16[16,2,2,128,128]{4,3,2,1,0:T(8,128)(2,1)}), bf16[16,2,2,128,128]{4,3,2,1,0:T(8,128)(2,1)S(1)}, u32[]{:S(2)}, u32[]{:S(2)}) %all-to-all-start.1) | async-done | bytes 2097184 | tf_op jit(solution)/shard_map/all_to_all | solution.py:199
  62.5 0.0 copy-done.2
  62.5 0.0 copy-start
  62.5 1.3 copy-done
  63.8 40.1 %shard_map.85 = (bf16[1024,1024]{1,0:T(8,128)(2,1)}, bf16[1024,1024]{1,0:T(8,128)(2,1)}, f32[8,2,128,128]{3,2,1,0:T(8,128)}, bf16[16,2,2,128,128]{4,3,2,1,0:T(8,128)(2,1)}, bf16[2,128,128]{2,1,0:T(8,128)(2,1)}) custom-call(s32[384]{0:T(512)} %reshape.20.rand, bf16[1024,1024]{1,0:T(8,128)(2,1)} %q_ref.1, bf16[1024,1024]{1,0:T(8,128)(2,1)} %g_ref.1, ...), custom_call_target="tpu_custom_call" | custom-call | tf_op jit(solution)/shard_map/pallas_call | solution.py:203
  103.9 0.0 copy-start.5
  103.9 4.7 %all-to-all-start.2 = ((bf16[16,2,2,128,128]{4,3,2,1,0:T(8,128)(2,1)}), bf16[16,2,2,128,128]{4,3,2,1,0:T(8,128)(2,1)S(1)}, u32[]{:S(2)}, u32[]{:S(2)}) async-start(bf16[16,2,2,128,128]{4,3,2,1,0:T(8,128)(2,1)} %get-tuple-element.12), calls=%async_computation.2 | async-start | bytes 4194304 | tf_op jit(solution)/shard_map/all_to_all | solution.py:242
  108.7 0.0 copy-done.5
  108.7 1.3 collective-permute-start.1
  110.0 26.1 %collective-permute-done.1.extra_ref = bf16[2,128,128]{2,1,0:T(8,128)(2,1)S(1)} collective-permute-done((bf16[2,128,128]{2,1,0:T(8,128)(2,1)S(1)}, bf16[2,128,128]{2,1,0:T(8,128)(2,1)S(1)}, u32[]{:S(2)}, u32[]{:S(2)}) %collective-permute-start.1) | collective-permute-done | bytes 65568 | tf_op jit(solution)/shard_map/ppermute | solution.py:243
  136.0 0.0 copy-start.3
  136.0 1.9 %all-to-all-done.2.back_ref = bf16[16,2,2,128,128]{4,3,2,1,0:T(8,128)(2,1)S(1)} async-done(((bf16[16,2,2,128,128]{4,3,2,1,0:T(8,128)(2,1)}), bf16[16,2,2,128,128]{4,3,2,1,0:T(8,128)(2,1)S(1)}, u32[]{:S(2)}, u32[]{:S(2)}) %all-to-all-start.2) | async-done | bytes 2097184 | tf_op jit(solution)/shard_map/all_to_all | solution.py:242
  137.9 0.0 copy-start.1
  137.9 0.0 copy-done.3
  137.9 1.3 copy-done.1
  139.2 6.5 %shard_map.86 = bf16[2,8,128,128]{3,2,1,0:T(8,128)(2,1)} custom-call(s32[384]{0:T(512)} %reshape.20.rand, f32[8,2,128,128]{3,2,1,0:T(8,128)} %get-tuple-element.11.local_ref, bf16[16,2,2,128,128]{4,3,2,1,0:T(8,128)(2,1)} %copy-done.1, bf16[2,128,128]{2,1,0:T(8,128)(2,1)} %copy-done.3), custom_call_target="tpu_custom_call" | custom-call | tf_op jit(solution)/shard_map/pallas_call | solution.py:244
  145.8 1.6 copy.35
  147.3 14.4 %all_to_all.40 = bf16[2,1024,128]{2,0,1:T(2,128)(2,1)S(1)} all-to-all(bf16[2,1024,128]{2,0,1:T(2,128)(2,1)S(1)} %copy.35), channel_id=1, replica_groups=mesh['ctx'=16,'kvh'=8] {'kvh'}, dimensions={1} | all-to-all | bytes 1048576 | tf_op jit(solution)/shard_map/all_to_all | solution.py:252
  161.7 0.9 fusion
  162.7 0.3 copy.37
  163.0 0.3 copy.36
  163.3 0.9 copy_bitcast_fusion
  (1 shorter events, 0.0 us)
Async XLA Ops:
  0.6 8.2 %copy-start.4 = (s32[128,3]{0,1:T(4,128)S(1)}, s32[128,3]{0,1:T(4,128)}, u32[]{:S(2)}) copy-start(s32[128,3]{0,1:T(4,128)} %param.9) | copy-start | bytes 4612
  2.8 15.3 %all-to-all-start = ((bf16[2,128,1024]{1,0,2:T(2,128)(2,1)}), bf16[2,128,1024]{1,0,2:T(2,128)(2,1)S(1)}, u32[]{:S(2)}, u32[]{:S(2)}) async-start(bf16[2,128,1024]{1,0,2:T(2,128)(2,1)} %copy.30), calls=%async_computation | async-start | bytes 1048576 | tf_op jit(solution)/shard_map/all_to_all | solution.py:189
  25.0 37.5 %all-to-all-start.1 = ((bf16[16,2,2,128,128]{4,3,2,1,0:T(8,128)(2,1)}), bf16[16,2,2,128,128]{4,3,2,1,0:T(8,128)(2,1)S(1)}, u32[]{:S(2)}, u32[]{:S(2)}) async-start(bf16[16,2,2,128,128]{4,3,2,1,0:T(8,128)(2,1)} %shard_map.84), calls=%async_computation.1 | async-start | bytes 4194304 | tf_op jit(solution)/shard_map/all_to_all | solution.py:199
  33.1 25.7 %collective-permute-start = (bf16[2,128,128]{2,1,0:T(8,128)(2,1)S(1)}, bf16[2,128,128]{2,1,0:T(8,128)(2,1)S(1)}, u32[]{:S(2)}, u32[]{:S(2)}) collective-permute-start(bf16[2,128,128]{2,1,0:T(8,128)(2,1)S(1)} %slice_bitcast_fusion), channel_id=1, source_target_pairs={{0,8},{1,9},{2,10},{3,11},{4,12},{5,13},{6,14},{7,15}} | collective-permute-start | bytes 196616 | tf_op jit(solution)/shard_map/ppermute | solution.py:191
  58.8 3.8 %copy-start.2 = (bf16[2,128,128]{2,1,0:T(8,128)(2,1)}, bf16[2,128,128]{2,1,0:T(8,128)(2,1)S(1)}, u32[]{:S(2)}) copy-start(bf16[2,128,128]{2,1,0:T(8,128)(2,1)S(1)} %collective-permute-done.extra_ref) | copy-start | bytes 196612
  62.5 1.3 copy-start
  103.9 4.7 %copy-start.5 = (bf16[2,128,128]{2,1,0:T(8,128)(2,1)S(1)}, bf16[2,128,128]{2,1,0:T(8,128)(2,1)}, u32[]{:S(2)}) copy-start(bf16[2,128,128]{2,1,0:T(8,128)(2,1)} %get-tuple-element.13) | copy-start | bytes 196612
  103.9 34.0 %all-to-all-start.2 = ((bf16[16,2,2,128,128]{4,3,2,1,0:T(8,128)(2,1)}), bf16[16,2,2,128,128]{4,3,2,1,0:T(8,128)(2,1)S(1)}, u32[]{:S(2)}, u32[]{:S(2)}) async-start(bf16[16,2,2,128,128]{4,3,2,1,0:T(8,128)(2,1)} %get-tuple-element.12), calls=%async_computation.2 | async-start | bytes 4194304 | tf_op jit(solution)/shard_map/all_to_all | solution.py:242
  108.7 27.4 %collective-permute-start.1 = (bf16[2,128,128]{2,1,0:T(8,128)(2,1)S(1)}, bf16[2,128,128]{2,1,0:T(8,128)(2,1)S(1)}, u32[]{:S(2)}, u32[]{:S(2)}) collective-permute-start(bf16[2,128,128]{2,1,0:T(8,128)(2,1)S(1)} %copy-done.5), channel_id=1, source_target_pairs={{8,0},{9,1},{10,2},{11,3},{12,4},{13,5},{14,6},{15,7}} | collective-permute-start | bytes 196616 | tf_op jit(solution)/shard_map/ppermute | solution.py:243
  136.0 1.9 %copy-start.3 = (bf16[2,128,128]{2,1,0:T(8,128)(2,1)}, bf16[2,128,128]{2,1,0:T(8,128)(2,1)S(1)}, u32[]{:S(2)}) copy-start(bf16[2,128,128]{2,1,0:T(8,128)(2,1)S(1)} %collective-permute-done.1.extra_ref) | copy-start | bytes 196612
  137.9 1.3 copy-start.1

commit v2 on v1

v2 whole, which is shorter than its diff:
```python
import functools

import jax
import jax.numpy as jnp
from jax import lax
from jax.experimental import pallas as pl
from jax.experimental.pallas import tpu as pltpu
from jax.sharding import PartitionSpec as P

HD = 128
BLK = 128
GLOB = 2
RAND = 3
QB = 8
CTX = 16
KVH = 8
HEADS = 8
SLOTS = 2
NKB = QB * CTX
SIDE = 4
EXTRA = QB
RECV = QB + 1
POOL = RECV + CTX * SLOTS
ENTRIES = 3 + GLOB + RAND
CHUNK = 512
SCALE = HD**-0.5
LOG2E = 1.4426950408889634
MASKED = -1e30
MESH = pl.DeviceIdType.MESH
ORDER = (
    (0, 1), (1, 0), (0, 3), (3, 0), (1, 1), (2, 0), (3, 3), (0, 2),
    (1, 3), (2, 1), (3, 1), (1, 2), (2, 3), (3, 2), (2, 2),
)

NT = (((1,), (1,)), ((), ()))
TN = (((0,), (0,)), ((), ()))


def mm(a, b, dims=(((1,), (0,)), ((), ()))):
    return lax.dot_general(a, b, dims, preferred_element_type=jnp.float32)


def ctx_at(me, dz, dx):
    return lax.rem(me // SIDE + dz, SIDE) * SIDE + lax.rem(me % SIDE + dx, SIDE)


def slot_table(rand, me, table):
    def body(dest, carry):
        first = second = count = jnp.int32(0)
        for e in range(QB * RAND):
            r = rand[dest * (QB * RAND) + e]
            hit = (r >> 3) == me
            first = jnp.where(hit & (count == 0), r & 7, first)
            second = jnp.where(hit & (count == 1), r & 7, second)
            count = count + hit.astype(jnp.int32)
        first = jnp.where(dest == me + 1, QB - 1, first)
        table[dest * 2] = jnp.where(me == 0, 0, first)
        table[dest * 2 + 1] = jnp.where(me == 0, 1, second)
        return carry

    lax.fori_loop(0, CTX, body, 0)


def greet(me, h):
    barrier = pltpu.get_barrier_semaphore()
    for dz, dx in ORDER:
        peer = (ctx_at(me, dz, dx), h)
        pl.semaphore_signal(barrier, inc=1, device_id=peer, device_id_type=MESH)
    for dh in range(1, KVH):
        peer = (me, lax.rem(h + dh, KVH))
        pl.semaphore_signal(barrier, inc=1, device_id=peer, device_id_type=MESH)
    pl.semaphore_wait(barrier, CTX + KVH - 2)


def remote(src, dst, send, recv, peer):
    return pltpu.make_async_remote_copy(
        src_ref=src, dst_ref=dst, send_sem=send, recv_sem=recv, device_id=peer, device_id_type=MESH
    )


def gather_kernel(
    rand, key_ref, value_ref, pool_ref, table_ref,
    local_k, local_v, packed, head_send, head_recv, ctx_send, ctx_recv, extra_sem, own_sem, keep_sem,
):
    me = lax.axis_index("ctx")
    h = lax.axis_index("kvh")
    greet(me, h)
    local = (local_k, local_v)
    cols = lambda head: pl.ds(pl.multiple_of(head * HD, HD), HD)
    head_copies = []
    own_copies = []
    for t, ref in enumerate((key_ref, value_ref)):
        for dh in range(1, KVH):
            peer = lax.rem(h + dh, KVH)
            head_copies.append(
                remote(
                    ref.at[:, cols(peer)], local[t].at[h],
                    head_send.at[t, peer], head_recv.at[t, h], (me, peer),
                )
            )
            head_copies[-1].start()
        own_copies.append(
            pltpu.make_async_copy(ref.at[:, cols(h)], local[t].at[h], own_sem.at[t])
        )
        own_copies[-1].start()
    slot_table(rand, me, table_ref)
    keep_copies = []
    ctx_copies = []
    for t in range(2):
        own_copies[t].wait()
        for dh in range(1, KVH):
            peer = lax.rem(h + dh, KVH)
            remote(
                local[t].at[peer], local[t].at[peer],
                head_send.at[t, peer], head_recv.at[t, peer], (me, peer),
            ).wait_recv()
        keep_copies.append(
            pltpu.make_async_copy(local[t], pool_ref.at[t, pl.ds(0, QB)], keep_sem.at[t])
        )
        keep_copies[-1].start()
        for dz, dx in ORDER:
            peer = ctx_at(me, dz, dx)
            for k in range(SLOTS):
                packed[t, peer, k] = local[t][table_ref[peer * 2 + k]]
        for dz, dx in ORDER:
            peer = ctx_at(me, dz, dx)
            ctx_copies.append(
                remote(
                    packed.at[t, peer], pool_ref.at[t, pl.ds(RECV + me * SLOTS, SLOTS)],
                    ctx_send.at[t, peer], ctx_recv.at[t, me], (peer, h),
                )
            )
            ctx_copies[-1].start()

    def extra(t):
        return remote(
            local[t].at[QB - 1], pool_ref.at[t, EXTRA], extra_sem.at[0, t], extra_sem.at[1, t], (1, h)
        )

    @pl.when(me == 0)
    def _():
        for t in range(2):
            extra(t).start()
        for t in range(2):
            extra(t).wait_send()

    @pl.when(me == 1)
    def _():
        for t in range(2):
            remote(
                local[t].at[QB - 1], pool_ref.at[t, EXTRA],
                extra_sem.at[0, t], extra_sem.at[1, t], (0, h),
            ).wait_recv()

    for copy in head_copies:
        copy.wait_send()
    for copy in keep_copies:
        copy.wait()
    for copy in ctx_copies:
        copy.wait_send()
    for t in range(2):
        for dz, dx in ORDER:
            peer = ctx_at(me, dz, dx)
            remote(
                packed.at[t, peer], pool_ref.at[t, pl.ds(RECV + peer * SLOTS, SLOTS)],
                ctx_send.at[t, peer], ctx_recv.at[t, peer], (peer, h),
            ).wait_recv()


def attend_kernel(
    rand, q_ref, g_ref, pool,
    o_ref, dq_ref, local_ref, back_ref, back_extra_ref,
    grads, kall, vall, dk, dv, table, fill,
):
    me = lax.axis_index("ctx")
    i = pl.program_id(0)

    @pl.when(i == 0)
    def _():
        grads[...] = jnp.zeros_like(grads)
        back_ref[...] = jnp.zeros_like(back_ref)
        for s in range(CTX):
            fill[s] = 0

    for e in range(3):
        gid = me * QB + i - 1 + e
        near = i - 1 + e
        before = jnp.where(me == 1, EXTRA, RECV + (me - 1) * SLOTS)
        after = RECV + (me + 1) * SLOTS
        place = jnp.where(near < 0, before, jnp.where(near >= QB, after, near))
        ok = (gid >= GLOB) & (gid < NKB)
        table[e] = jnp.where(ok, place, 0)
    for e in range(GLOB):
        table[3 + e] = jnp.where(me == 0, e, RECV + e)
    for e in range(RAND):
        r = rand[(me * QB + i) * RAND + e]
        owner = r >> 3
        rank = fill[owner]
        fill[owner] = rank + 1
        table[3 + GLOB + e] = RECV + owner * SLOTS + rank

    for e in range(ENTRIES):
        kall[e * BLK : (e + 1) * BLK, :] = pool[0, table[e]]
        vall[e * BLK : (e + 1) * BLK, :] = pool[1, table[e]]
    dk[...] = jnp.zeros_like(dk)
    dv[...] = jnp.zeros_like(dv)
    per = CHUNK // BLK

    def chunk(j, carry):
        cols = [pl.ds(pl.multiple_of((j * per + t) * HD, HD), HD) for t in range(per)]
        q = jnp.concatenate([q_ref[:, c] for c in cols], 0)
        g = jnp.concatenate([g_ref[:, c] for c in cols], 0)
        s = mm(q, kall[...], NT)
        parts = []
        for e in range(ENTRIES):
            part = s[:, e * BLK : (e + 1) * BLK]
            if e < 3:
                gid = me * QB + i - 1 + e
                ok = (gid >= GLOB) & (gid < NKB)
                part = part + jnp.where(ok, 0.0, MASKED).astype(jnp.float32)
            parts.append(part)
        s = jnp.concatenate(parts, 1)
        top = jnp.max(s, 1, keepdims=True)
        p = jnp.exp2(s * (SCALE * LOG2E) - top * (SCALE * LOG2E))
        inv = 1.0 / jnp.sum(p, 1, keepdims=True)
        pb = p.astype(jnp.bfloat16)
        o = mm(pb, vall[...]) * inv
        gb = (g.astype(jnp.float32) * inv).astype(jnp.bfloat16)
        centre = jnp.sum(gb.astype(jnp.float32) * o, 1, keepdims=True)
        dp = mm(gb, vall[...], NT)
        ds = (p * (dp - centre)).astype(jnp.bfloat16)
        dq = mm(ds, kall[...]) * SCALE
        for t in range(per):
            rows = slice(t * BLK, (t + 1) * BLK)
            o_ref[:, cols[t]] = o[rows].astype(jnp.bfloat16)
            dq_ref[:, cols[t]] = dq[rows].astype(jnp.bfloat16)
        dv[...] += mm(gb, pb, TN)
        dk[...] += mm(q, ds, TN)
        return carry

    lax.fori_loop(0, HEADS * BLK // CHUNK, chunk, 0)
    for e in range(ENTRIES):
        cols = slice(e * BLK, (e + 1) * BLK)
        key_part = dk[:, cols] * SCALE
        value_part = dv[:, cols]
        if e < 3 + GLOB:
            grads[0, table[e]] += key_part
            grads[1, table[e]] += value_part
        else:
            slot = table[e] - RECV
            back_ref[0, slot] = key_part.astype(jnp.bfloat16)
            back_ref[1, slot] = value_part.astype(jnp.bfloat16)

    @pl.when(i == QB - 1)
    def _():
        for t in range(2):
            for b in range(QB):
                local_ref[t, b] = grads[t, b]
            back_extra_ref[t] = grads[t, EXTRA].astype(jnp.bfloat16)

        def shared(src):
            for t in range(2):
                for k in range(SLOTS):
                    slot = src * SLOTS + k
                    back_ref[t, slot] = grads[t, RECV + slot].astype(jnp.bfloat16)

        pl.when(me != 0)(lambda: shared(0))
        pl.when(me > 1)(lambda: shared(me - 1))
        pl.when(me < CTX - 1)(lambda: shared(me + 1))


def scatter_kernel(
    table, local_ref, back_ref, extra_ref, dk_ref, dv_ref,
    acc, arrived, extra_in, stage, ctx_send, ctx_recv, head_send, head_recv, extra_sem, own_sem,
):
    me = lax.axis_index("ctx")
    h = lax.axis_index("kvh")
    greet(me, h)
    ctx_copies = []
    for t in (1, 0):
        for dz, dx in ORDER:
            peer = ctx_at(me, dz, dx)
            ctx_copies.append(
                remote(
                    back_ref.at[t, pl.ds(peer * SLOTS, SLOTS)], arrived.at[t, me],
                    ctx_send.at[t, peer], ctx_recv.at[t, me], (peer, h),
                )
            )
            ctx_copies[-1].start()

    def extra(t, peer):
        return remote(extra_ref.at[t], extra_in.at[t], extra_sem.at[0, t], extra_sem.at[1, t], (peer, h))

    @pl.when(me == 1)
    def _():
        for t in range(2):
            extra(t, 0).start()

    acc[...] = local_ref[...]
    cols = lambda head: pl.ds(pl.multiple_of(head * HD, HD), HD)
    head_copies = []
    own_copies = []
    for t, ref in ((1, dv_ref), (0, dk_ref)):

        def body(n, carry):
            peer = lax.rem(me + n, CTX)
            remote(
                back_ref.at[t, pl.ds(peer * SLOTS, SLOTS)], arrived.at[t, peer],
                ctx_send.at[t, peer], ctx_recv.at[t, peer], (peer, h),
            ).wait_recv()
            for k in range(SLOTS):
                place = table[peer * 2 + k]
                term = arrived[t, peer, k].astype(jnp.float32)
                for b in range(QB):
                    acc[t, b] += term * (place == b).astype(jnp.float32)
            return carry

        lax.fori_loop(1, CTX, body, 0)

        @pl.when(me == 0)
        def _():
            extra(t, 1).wait_recv()
            acc[t, QB - 1] += extra_in[t].astype(jnp.float32)

        for b in range(QB):
            stage[t, b] = acc[t, b].T.astype(jnp.bfloat16)
        for dh in range(1, KVH):
            peer = lax.rem(h + dh, KVH)
            head_copies.append(
                remote(
                    stage.at[t, peer], ref.at[:, cols(h)],
                    head_send.at[t, peer], head_recv.at[t, h], (me, peer),
                )
            )
            head_copies[-1].start()
        own_copies.append(pltpu.make_async_copy(stage.at[t, h], ref.at[:, cols(h)], own_sem.at[t]))
        own_copies[-1].start()

    @pl.when(me == 1)
    def _():
        for t in range(2):
            extra(t, 0).wait_send()

    for copy in ctx_copies:
        copy.wait_send()
    for copy in own_copies:
        copy.wait()
    for copy in head_copies:
        copy.wait_send()
    for t, ref in ((1, dv_ref), (0, dk_ref)):
        for dh in range(1, KVH):
            peer = lax.rem(h + dh, KVH)
            remote(
                stage.at[t, peer], ref.at[:, cols(peer)],
                head_send.at[t, peer], head_recv.at[t, peer], (me, peer),
            ).wait_recv()


VM = pl.BlockSpec(memory_space=pltpu.VMEM)
SM = pl.BlockSpec(memory_space=pltpu.SMEM)
ANY = pl.BlockSpec(memory_space=pl.ANY)
DMA = pltpu.SemaphoreType.DMA
VMEM_BYTES = 56 * 2**20


def per_device(queries, keys, values, out_grad, random_blocks):
    rand = random_blocks.reshape(-1)
    bf = jnp.bfloat16
    pool, table = pl.pallas_call(
        gather_kernel,
        out_shape=[
            jax.ShapeDtypeStruct((2, POOL, BLK, HD), bf),
            jax.ShapeDtypeStruct((CTX * SLOTS,), jnp.int32),
        ],
        in_specs=[SM, ANY, ANY],
        out_specs=[ANY, SM],
        scratch_shapes=[
            pltpu.VMEM((QB, BLK, HD), bf),
            pltpu.VMEM((QB, BLK, HD), bf),
            pltpu.VMEM((2, CTX, SLOTS, BLK, HD), bf),
            DMA((2, KVH)), DMA((2, KVH)), DMA((2, CTX)), DMA((2, CTX)), DMA((2, 2)), DMA((2,)), DMA((2,)),
        ],
        compiler_params=pltpu.CompilerParams(
            collective_id=0, has_side_effects=True, vmem_limit_bytes=VMEM_BYTES
        ),
    )(rand, keys, values)
    whole = lambda shape: pl.BlockSpec(shape, lambda i, *_: (0,) * len(shape))
    rows = pl.BlockSpec((BLK, HEADS * HD), lambda i, *_: (i, 0))
    tok = QB * BLK
    attended, query_grad, local, back, back_extra = pl.pallas_call(
        attend_kernel,
        grid_spec=pltpu.PrefetchScalarGridSpec(
            num_scalar_prefetch=1,
            grid=(QB,),
            in_specs=[rows, rows, whole((2, POOL, BLK, HD))],
            out_specs=[
                rows,
                rows,
                whole((2, QB, HD, BLK)),
                whole((2, CTX * SLOTS, HD, BLK)),
                whole((2, HD, BLK)),
            ],
            scratch_shapes=[
                pltpu.VMEM((2, POOL, HD, BLK), jnp.float32),
                pltpu.VMEM((ENTRIES * BLK, HD), bf),
                pltpu.VMEM((ENTRIES * BLK, HD), bf),
                pltpu.VMEM((HD, ENTRIES * BLK), jnp.float32),
                pltpu.VMEM((HD, ENTRIES * BLK), jnp.float32),
                pltpu.SMEM((ENTRIES,), jnp.int32),
                pltpu.SMEM((CTX,), jnp.int32),
            ],
        ),
        out_shape=[
            jax.ShapeDtypeStruct((tok, HEADS * HD), bf),
            jax.ShapeDtypeStruct((tok, HEADS * HD), bf),
            jax.ShapeDtypeStruct((2, QB, HD, BLK), jnp.float32),
            jax.ShapeDtypeStruct((2, CTX * SLOTS, HD, BLK), bf),
            jax.ShapeDtypeStruct((2, HD, BLK), bf),
        ],
        compiler_params=pltpu.CompilerParams(vmem_limit_bytes=VMEM_BYTES),
    )(rand, queries, out_grad, pool)
    key_grad, value_grad = pl.pallas_call(
        scatter_kernel,
        out_shape=[jax.ShapeDtypeStruct((BLK, KVH * HD), bf)] * 2,
        in_specs=[SM, VM, ANY, ANY],
        out_specs=[ANY, ANY],
        scratch_shapes=[
            pltpu.VMEM((2, QB, HD, BLK), jnp.float32),
            pltpu.VMEM((2, CTX, SLOTS, HD, BLK), bf),
            pltpu.VMEM((2, HD, BLK), bf),
            pltpu.VMEM((2, QB, BLK, HD), bf),
            DMA((2, CTX)), DMA((2, CTX)), DMA((2, KVH)), DMA((2, KVH)), DMA((2, 2)), DMA((2,)),
        ],
        compiler_params=pltpu.CompilerParams(
            collective_id=1, has_side_effects=True, vmem_limit_bytes=VMEM_BYTES
        ),
    )(table, local, back, back_extra)
    return attended, query_grad, key_grad, value_grad


def solution(mesh):
    in_specs = (
        P("ctx", "kvh"),
        P(("ctx", "kvh"), None),
        P(("ctx", "kvh"), None),
        P("ctx", "kvh"),
        P(),
    )
    out_specs = (P("ctx", "kvh"), P("ctx", "kvh"), P(("ctx", "kvh"), None), P(("ctx", "kvh"), None))
    return jax.shard_map(
        per_device, mesh=mesh, in_specs=in_specs, out_specs=out_specs, check_vma=False
    )
```

time: 165 us -> 130 us (0.79)
  Pallas kernels: 52.4 us -> 124 us
  waiting for transfers between devices: 62.5 us -> 0 us
  starting transfers between devices: 22.8 us -> 0 us
  blocking collectives: 14.4 us -> 0 us
  local copies, waits for them, and re-layouts: 10.2 us -> 4.91 us
    pallas_call x2, Pallas kernels: 12.3 us -> 84.1 us  [the longest x1 44.6 us: per_device(): pl.pallas_call(gather_kernel, out_shape=[jax.ShapeDtypeStruct((2, POOL, B...]
    ppermute x2 -> x0, waiting for transfers between devices: 48.5 us -> none  [the longest x1 26.1 us: per_device(): back_extra = lax.ppermute(back_extra, 'ctx', [(1, 0)])]
    all_to_all x3 -> x0, starting transfers between devices: 18.3 us -> none  [the longest x1 7.6 us: per_device(): recv = lax.all_to_all(send, 'ctx', split_axis=0, concat_axis=0, tiled=True)]
    all_to_all x1 -> x0, blocking collectives: 14.4 us -> none  [per_device(): lax.all_to_all(total.reshape(2, tok, HD), 'kvh', split_axis=1, concat_axi...]
    all_to_all x3 -> x0, waiting for transfers between devices: 14.1 us -> none  [the longest x1 8.45 us: per_device(): kv = lax.all_to_all(stacked, 'kvh', split_axis=2, concat_axis=1, tiled=True)]
    ppermute x2 -> x0, starting transfers between devices: 4.56 us -> none  [the longest x1 3.26 us: per_device(): extra = lax.ppermute(kv[:, QB - 1], 'ctx', [(0, 1)])]
    unnamed x13 -> x3, local copies, waits for them, and re-layouts: 2.79 us -> 4.13 us
  transfers between devices with their start and end apart: 5 -> 0, of which waited for: 5 -> 0; matrix products, arithmetic and copies ran while one was open for 1% -> 0% of each run, Pallas kernels for 0% -> 0%
where the time goes in v2:
time: 130 us; the launch traced here: 129 us
  Pallas kernels  124 us (95%)
  local copies, waits for them, and re-layouts  4.91 us (4%)
    pallas_call x1, Pallas kernels, per_device(): pl.pallas_call(gather_kernel, out_shape=[jax.ShapeDtypeStruct((2, POOL, B...  44.6 us
    pallas_call x1, Pallas kernels, per_device(): pl.pallas_call(attend_kernel, grid_spec=pltpu.PrefetchScalarGridSpec(num_...  39.8 us
    pallas_call x1, Pallas kernels, per_device(): pl.pallas_call(scatter_kernel, out_shape=[jax.ShapeDtypeStruct((BLK, KVH...  39.5 us
    unnamed x3, local copies, waits for them, and re-layouts  4.13 us

profile of v2, /device:TPU:1, one launch (start us, length us, event | category | flops | bytes accessed | tf_op | source)
XLA Modules:
  0.0 129.4 jit_solution(8490942685929833283)
XLA Ops:
  0.6 0.8 copy.9
  1.4 0.8 reshape.11.rand
  2.2 44.6 %shard_map.84 = (bf16[2,41,128,128]{3,2,1,0:T(8,128)(2,1)}, s32[32]{0:T(128)}) custom-call(s32[384]{0:T(512)} %reshape.11.rand, bf16[128,1024]{1,0:T(8,128)(2,1)} %key_ref.1, bf16[128,1024]{1,0:T(8,128)(2,1)} %value_ref.1), custom_call_target="tpu_custom_call" | custom-call | tf_op jit(solution)/shard_map/pallas_call | solution.py:369
  46.8 39.8 %shard_map.85 = (bf16[1024,1024]{1,0:T(8,128)(2,1)}, bf16[1024,1024]{1,0:T(8,128)(2,1)}, f32[2,8,128,128]{3,2,1,0:T(8,128)}, bf16[2,32,128,128]{3,2,1,0:T(8,128)(2,1)}, bf16[2,128,128]{2,1,0:T(8,128)(2,1)}) custom-call(s32[384]{0:T(512)} %reshape.11.rand, bf16[1024,1024]{1,0:T(8,128)(2,1)} %q_ref.1, bf16[1024,1024]{1,0:T(8,128)(2,1)} %g_ref.1, ...), custom_call_target="tpu_custom_call" | custom-call | tf_op jit(solution)/shard_map/pallas_call | solution.py:390
  86.6 39.5 %shard_map.86 = (bf16[128,1024]{1,0:T(8,128)(2,1)}, bf16[128,1024]{1,0:T(8,128)(2,1)}) custom-call(s32[32]{0:T(128)} %get-tuple-element.16.table, f32[2,8,128,128]{3,2,1,0:T(8,128)} %get-tuple-element.17.local_ref, bf16[2,32,128,128]{3,2,1,0:T(8,128)(2,1)} %get-tuple-element.18.back_ref, bf16[2,128,128]{2,1,0:T(8,128)(2,1)} %get-tuple-element.19.extra_ref), custom_call_target="tpu_custom_call" | custom-call | tf_op jit(solution)/shard_map/pallas_call | solution.py:422
  126.1 1.7 %copy.12 = bf16[128,1024]{1,0:T(8,128)(2,1)} copy(bf16[128,1024]{1,0:T(8,128)(2,1)} %get-tuple-element.28) | data formatting | bytes 524288
  127.7 1.7 %copy.13 = bf16[128,1024]{1,0:T(8,128)(2,1)} copy(bf16[128,1024]{1,0:T(8,128)(2,1)} %get-tuple-element.29) | data formatting | bytes 524288

commit v3 on v0

v3 whole, which is shorter than its diff:
```python
import functools

import jax
import jax.numpy as jnp
from jax import lax
from jax.experimental import pallas as pl
from jax.experimental.pallas import tpu as pltpu
from jax.sharding import PartitionSpec as P

HD = 128
BLK = 128
GLOB = 2
RAND = 3
QB = 8
CTX = 16
KVH = 8
HEADS = 8
SLOTS = 2
NKB = QB * CTX
SIDE = 4
EXTRA = QB
RECV = QB + 1
POOL = RECV + CTX * SLOTS
ENTRIES = 3 + GLOB + RAND
CHUNK = 512
PER = CHUNK // BLK
HALVES = HEADS // PER
NAMED = QB * RAND
EDGE = NAMED + GLOB
NONE = EDGE + 2
SUMS = QB + 2 + GLOB
SCALE = HD**-0.5
LOG2E = 1.4426950408889634
MASKED = -1e30
MESH = pl.DeviceIdType.MESH
ORDER = (
    (0, 1), (1, 0), (0, 3), (3, 0), (1, 1), (2, 0), (3, 3), (0, 2),
    (1, 3), (2, 1), (3, 1), (1, 2), (2, 3), (3, 2), (2, 2),
)

NT = (((1,), (1,)), ((), ()))
TN = (((0,), (0,)), ((), ()))


def mm(a, b, dims=(((1,), (0,)), ((), ()))):
    return lax.dot_general(a, b, dims, preferred_element_type=jnp.float32)


def ctx_at(me, dz, dx):
    return lax.rem(me // SIDE + dz, SIDE) * SIDE + lax.rem(me % SIDE + dx, SIDE)


def pick(rand, row, owner, name):
    first = second = jnp.int32(name(None, None))
    count = jnp.int32(0)
    for n in range(NAMED):
        r = rand[row * NAMED + n]
        hit = (r >> 3) == owner
        first = jnp.where(hit & (count == 0), name(r, n), first)
        second = jnp.where(hit & (count == 1), name(r, n), second)
        count = count + hit.astype(jnp.int32)
    return first, second


def send_table(rand, me, table):
    def body(dest, carry):
        first, second = pick(rand, dest, me, lambda r, n: 0 if r is None else r & 7)
        first = jnp.where(dest == me + 1, QB - 1, first)
        table[dest * 2] = jnp.where(me == 0, 0, first)
        table[dest * 2 + 1] = jnp.where(me == 0, 1, second)
        return carry

    lax.fori_loop(0, CTX, body, 0)


def back_table(rand, me, table):
    def body(src, carry):
        first, second = pick(rand, me, src, lambda r, n: NONE if r is None else n)
        first = jnp.where(src == me - 1, EDGE, first)
        first = jnp.where(src == me + 1, EDGE + 1, first)
        table[src * 2] = jnp.where(src == 0, NAMED, first)
        table[src * 2 + 1] = jnp.where(src == 0, NAMED + 1, second)
        return carry

    lax.fori_loop(0, CTX, body, 0)


def place_table(rand, me, table):
    def body(i, carry):
        for e in range(3):
            gid = me * QB + i - 1 + e
            near = i - 1 + e
            before = jnp.where(me == 1, EXTRA, RECV + (me - 1) * SLOTS)
            after = RECV + (me + 1) * SLOTS
            place = jnp.where(near < 0, before, jnp.where(near >= QB, after, near))
            ok = (gid >= GLOB) & (gid < NKB)
            table[i * ENTRIES + e] = jnp.where(ok, place, 0)
        for e in range(GLOB):
            table[i * ENTRIES + 3 + e] = jnp.where(me == 0, e, RECV + e)
        for e in range(RAND):
            owner = rand[me * NAMED + i * RAND + e] >> 3
            rank = jnp.int32(0)
            for n in range(NAMED):
                same = ((rand[me * NAMED + n] >> 3) == owner) & (n < i * RAND + e)
                rank = rank + same.astype(jnp.int32)
            table[i * ENTRIES + 3 + GLOB + e] = RECV + owner * SLOTS + rank
        return carry

    lax.fori_loop(0, QB, body, 0)


def greet(me, h):
    barrier = pltpu.get_barrier_semaphore()
    for dz, dx in ORDER:
        peer = (ctx_at(me, dz, dx), h)
        pl.semaphore_signal(barrier, inc=1, device_id=peer, device_id_type=MESH)
    for dh in range(1, KVH):
        peer = (me, lax.rem(h + dh, KVH))
        pl.semaphore_signal(barrier, inc=1, device_id=peer, device_id_type=MESH)
    pl.semaphore_wait(barrier, CTX + KVH - 2)


def remote(src, dst, send, recv, peer):
    return pltpu.make_async_remote_copy(
        src_ref=src, dst_ref=dst, send_sem=send, recv_sem=recv, device_id=peer, device_id_type=MESH
    )


def step_kernel(
    rand, q_hbm, g_hbm, key_ref, value_ref,
    o_hbm, dq_hbm, dk_ref, dv_ref,
    q, g, o, dq, probs, inverse, local_k, local_v, pool_k, pool_v, packed_k, packed_v, back_k, back_v,
    arrived_k, arrived_v, terms_k, terms_v, sums_k, sums_v, stage_k, stage_v, extra_k, extra_v,
    listed, part, outgoing, returning, places,
    head_send, head_recv, ctx_send, ctx_recv, home_send, home_recv, ret_send, ret_recv,
    extra_send, extra_recv, own_sem, home_own, in_sem, out_sem,
):
    me = lax.axis_index("ctx")
    h = lax.axis_index("kvh")
    bf = jnp.bfloat16
    pools, packs, backs = (pool_k, pool_v), (packed_k, packed_v), (back_k, back_v)
    local = (local_k, local_v)
    arrived, terms, sums = (arrived_k, arrived_v), (terms_k, terms_v), (sums_k, sums_v)
    stages, extras = (stage_k, stage_v), (extra_k, extra_v)
    loads = [
        pltpu.make_async_copy(q_hbm, q, in_sem.at[0]),
        pltpu.make_async_copy(g_hbm, g, in_sem.at[1]),
    ]
    for copy in loads:
        copy.start()
    greet(me, h)
    cols = lambda head: pl.ds(pl.multiple_of(head * HD, HD), HD)
    heads = lambda: [(dh, lax.rem(h + dh, KVH)) for dh in range(1, KVH)]
    peers = lambda: [ctx_at(me, dz, dx) for dz, dx in ORDER]
    sent = []
    own = []
    for t, ref in enumerate((key_ref, value_ref)):
        for _, peer in heads():
            sent.append(
                remote(
                    ref.at[:, cols(peer)], local[t].at[h],
                    head_send.at[t, peer], head_recv.at[t, h], (me, peer),
                )
            )
            sent[-1].start()
        own.append(pltpu.make_async_copy(ref.at[:, cols(h)], local[t].at[h], own_sem.at[t]))
        own[-1].start()
    send_table(rand, me, outgoing)
    for t in range(2):
        own[t].wait()
        for _, peer in heads():
            remote(
                local[t].at[peer], local[t].at[peer],
                head_send.at[t, peer], head_recv.at[t, peer], (me, peer),
            ).wait_recv()
        for peer in peers():
            for k in range(SLOTS):
                packs[t][peer, k] = local[t][outgoing[peer * 2 + k]]
        for peer in peers():
            sent.append(
                remote(
                    packs[t].at[peer], pools[t].at[pl.ds(RECV + me * SLOTS, SLOTS)],
                    ctx_send.at[t, peer], ctx_recv.at[t, me], (peer, h),
                )
            )
            sent[-1].start()

        @pl.when(me == 0)
        def _():
            remote(
                local[t].at[QB - 1], pools[t].at[EXTRA], extra_send.at[t], extra_recv.at[t], (1, h)
            ).start()

    place_table(rand, me, places)
    back_table(rand, me, returning)
    for t in range(2):
        for b in range(QB):
            pools[t][b] = local[t][b]
        sums[t][...] = jnp.zeros_like(sums[t])
        terms[t][NONE] = jnp.zeros((HD, BLK), bf)
    for copy in loads:
        copy.wait()

    def arrive(t):
        for peer in peers():
            remote(
                packs[t].at[peer], pools[t].at[pl.ds(RECV + peer * SLOTS, SLOTS)],
                ctx_send.at[t, peer], ctx_recv.at[t, peer], (peer, h),
            ).wait_recv()

        @pl.when(me == 1)
        def _():
            remote(
                local[t].at[QB - 1], pools[t].at[EXTRA], extra_send.at[t], extra_recv.at[t], (0, h)
            ).wait_recv()

    def collect(t, i):
        for e in range(ENTRIES):
            listed[e * BLK : (e + 1) * BLK, :] = pools[t][places[i * ENTRIES + e]]

    def rows_of(i, j):
        rows = pl.ds(pl.multiple_of(i * BLK, BLK), BLK)
        return [(rows, slice((j * PER + n) * HD, (j * PER + n + 1) * HD)) for n in range(PER)]

    def stacked(ref, where):
        return jnp.concatenate([ref[w] for w in where], 0)

    def spread(ref, where, value):
        for n, w in enumerate(where):
            ref[w] = value[n * BLK : (n + 1) * BLK].astype(bf)

    def bank(t, i, factor):
        for e in range(ENTRIES):
            term = part[:, e * BLK : (e + 1) * BLK] * factor
            if e < 3:
                sums[t][i + e] += term
            elif e < 3 + GLOB:
                sums[t][QB + 2 + e - 3] += term
            else:
                terms[t][i * RAND + e - 3 - GLOB] = term.astype(bf)

    def give_back(t):
        for n in range(GLOB):
            terms[t][NAMED + n] = sums[t][QB + 2 + n].astype(bf)
        terms[t][EDGE] = sums[t][0].astype(bf)
        terms[t][EDGE + 1] = sums[t][QB + 1].astype(bf)

        @pl.when(me == 0)
        def _():
            for n in range(GLOB):
                sums[t][1 + n] += sums[t][QB + 2 + n]

        for peer in peers():
            for k in range(SLOTS):
                backs[t][peer, k] = terms[t][returning[peer * 2 + k]]
        for peer in peers():
            sent.append(
                remote(
                    backs[t].at[peer], arrived[t].at[me],
                    ret_send.at[t, peer], ret_recv.at[t, me], (peer, h),
                )
            )
            sent[-1].start()

        @pl.when(me == 1)
        def _():
            remote(terms[t].at[EDGE], extras[t], extra_send.at[t], extra_recv.at[t], (0, h)).start()

    def finish(t, ref):
        def body(n, carry):
            peer = lax.rem(me + n, CTX)
            remote(
                backs[t].at[peer], arrived[t].at[peer],
                ret_send.at[t, peer], ret_recv.at[t, peer], (peer, h),
            ).wait_recv()
            for k in range(SLOTS):
                place = outgoing[peer * 2 + k]
                term = arrived[t][peer, k].astype(jnp.float32)
                for b in range(QB):
                    sums[t][1 + b] += term * (place == b).astype(jnp.float32)
            return carry

        lax.fori_loop(1, CTX, body, 0)

        @pl.when(me == 0)
        def _():
            remote(terms[t].at[EDGE], extras[t], extra_send.at[t], extra_recv.at[t], (1, h)).wait_recv()
            sums[t][QB] += extras[t][...].astype(jnp.float32)

        for b in range(QB):
            stages[t][b] = sums[t][1 + b].T.astype(bf)
        for _, peer in heads():
            sent.append(
                remote(
                    stages[t].at[peer], ref.at[:, cols(h)],
                    home_send.at[t, peer], home_recv.at[t, h], (me, peer),
                )
            )
            sent[-1].start()
        own.append(pltpu.make_async_copy(stages[t].at[h], ref.at[:, cols(h)], home_own.at[t]))
        own[-1].start()

    arrive(0)

    def weigh(i, carry):
        collect(0, i)
        for j in range(HALVES):
            where = rows_of(i, j)
            s = mm(stacked(q, where), listed[...], NT)
            parts = []
            for e in range(ENTRIES):
                piece = s[:, e * BLK : (e + 1) * BLK]
                if e < 3:
                    gid = me * QB + i - 1 + e
                    ok = (gid >= GLOB) & (gid < NKB)
                    piece = piece + jnp.where(ok, 0.0, MASKED).astype(jnp.float32)
                parts.append(piece)
            s = jnp.concatenate(parts, 1)
            top = jnp.max(s, 1, keepdims=True)
            p = jnp.exp2(s * (SCALE * LOG2E) - top * (SCALE * LOG2E))
            inv = 1.0 / jnp.sum(p, 1, keepdims=True)
            pb = p.astype(bf)
            gb = (stacked(g, where).astype(jnp.float32) * inv).astype(bf)
            probs[i * HALVES + j] = pb
            inverse[i * HALVES + j] = inv
            spread(g, where, gb)
            more = mm(gb, pb, TN)
            part[...] = more if j == 0 else part[...] + more
        bank(1, i, 1.0)
        return carry

    lax.fori_loop(0, QB, weigh, 0)
    give_back(1)
    arrive(1)

    def blame(i, carry):
        collect(1, i)
        for j in range(HALVES):
            where = rows_of(i, j)
            pb = probs[i * HALVES + j]
            gb = stacked(g, where)
            out = mm(pb, listed[...]) * inverse[i * HALVES + j]
            spread(o, where, out)
            centre = jnp.sum(gb.astype(jnp.float32) * out, 1, keepdims=True)
            dp = mm(gb, listed[...], NT)
            ds = (pb.astype(jnp.float32) * (dp - centre)).astype(bf)
            probs[i * HALVES + j] = ds
            more = mm(stacked(q, where), ds, TN)
            part[...] = more if j == 0 else part[...] + more
        bank(0, i, SCALE)
        return carry

    lax.fori_loop(0, QB, blame, 0)
    give_back(0)
    stores = [pltpu.make_async_copy(o, o_hbm, out_sem.at[0])]
    stores[-1].start()
    finish(1, dv_ref)

    def steer(i, carry):
        collect(0, i)
        for j in range(HALVES):
            spread(dq, rows_of(i, j), mm(probs[i * HALVES + j], listed[...]) * SCALE)
        return carry

    lax.fori_loop(0, QB, steer, 0)
    stores.append(pltpu.make_async_copy(dq, dq_hbm, out_sem.at[1]))
    stores[-1].start()
    finish(0, dk_ref)
    for t in range(2):

        @pl.when(me == 0)
        def _():
            remote(
                local[t].at[QB - 1], pools[t].at[EXTRA], extra_send.at[t], extra_recv.at[t], (1, h)
            ).wait_send()

        @pl.when(me == 1)
        def _():
            remote(terms[t].at[EDGE], extras[t], extra_send.at[t], extra_recv.at[t], (0, h)).wait_send()

    for copy in sent:
        copy.wait_send()
    for copy in own[2:] + stores:
        copy.wait()
    for t, ref in ((1, dv_ref), (0, dk_ref)):
        for _, peer in heads():
            remote(
                stages[t].at[peer], ref.at[:, cols(peer)],
                home_send.at[t, peer], home_recv.at[t, peer], (me, peer),
            ).wait_recv()


SM = pl.BlockSpec(memory_space=pltpu.SMEM)
ANY = pl.BlockSpec(memory_space=pl.ANY)
DMA = pltpu.SemaphoreType.DMA
VMEM_BYTES = 60 * 2**20


def per_device(queries, keys, values, out_grad, random_blocks):
    bf = jnp.bfloat16
    f32 = jnp.float32
    tok = QB * BLK
    big = pltpu.VMEM((tok, HEADS * HD), bf)
    slots = pltpu.VMEM((CTX, SLOTS, BLK, HD), bf)
    two = lambda shape, kind: [pltpu.VMEM(shape, kind)] * 2
    wide = jax.ShapeDtypeStruct((tok, HEADS * HD), bf)
    home = jax.ShapeDtypeStruct((BLK, KVH * HD), bf)
    return pl.pallas_call(
        step_kernel,
        out_shape=[wide, wide, home, home],
        in_specs=[SM, ANY, ANY, ANY, ANY],
        out_specs=[ANY] * 4,
        scratch_shapes=[big] * 4
        + [
            pltpu.VMEM((QB * HALVES, CHUNK, ENTRIES * BLK), bf),
            pltpu.VMEM((QB * HALVES, CHUNK, 1), f32),
        ]
        + two((QB, BLK, HD), bf)
        + two((POOL, BLK, HD), bf)
        + [slots] * 6
        + two((NONE + 1, HD, BLK), bf)
        + two((SUMS, HD, BLK), f32)
        + two((QB, BLK, HD), bf)
        + two((HD, BLK), bf)
        + [
            pltpu.VMEM((ENTRIES * BLK, HD), bf),
            pltpu.VMEM((HD, ENTRIES * BLK), f32),
            pltpu.SMEM((CTX * SLOTS,), jnp.int32),
            pltpu.SMEM((CTX * SLOTS,), jnp.int32),
            pltpu.SMEM((QB * ENTRIES,), jnp.int32),
        ]
        + [DMA((2, KVH))] * 2
        + [DMA((2, CTX))] * 2
        + [DMA((2, KVH))] * 2
        + [DMA((2, CTX))] * 2
        + [DMA((2,))] * 6,
        compiler_params=pltpu.CompilerParams(
            collective_id=0, has_side_effects=True, vmem_limit_bytes=VMEM_BYTES
        ),
    )(random_blocks.reshape(-1), queries, out_grad, keys, values)


def solution(mesh):
    in_specs = (
        P("ctx", "kvh"),
        P(("ctx", "kvh"), None),
        P(("ctx", "kvh"), None),
        P("ctx", "kvh"),
        P(),
    )
    out_specs = (P("ctx", "kvh"), P("ctx", "kvh"), P(("ctx", "kvh"), None), P(("ctx", "kvh"), None))
    return jax.shard_map(
        per_device, mesh=mesh, in_specs=in_specs, out_specs=out_specs, check_vma=False
    )
```

time: 479 us -> 100 us (0.21)
  waiting for transfers between devices: 155 us -> 0 us
  local copies, waits for them, and re-layouts: 119 us -> 7.54 us
  matrix products: 109 us -> 0 us
  Pallas kernels: 0 us -> 91.7 us
  other arithmetic: 56.6 us -> 0 us
  blocking collectives: 15.1 us -> 0 us
  between operations: 14.2 us -> 0.65 us
  starting transfers between devices: 6.46 us -> 0 us
    dot_general x48 -> x0, matrix products: 109 us -> none  [the longest x8 30.4 us: attend_block(): jnp.einsum('bgqd,kgd->gqbk', grad_rows, value_rows, preferred_element_typ...]
    pallas_call x0 -> x1, Pallas kernels: none -> 91.7 us  [per_device(): pl.pallas_call(step_kernel, out_shape=[wide, wide, home, home], in_specs=...]
    reduce_scatter x1 -> x0, waiting for transfers between devices: 84.4 us -> none  [per_device(): lax.psum_scatter(placed_rows.astype(jnp.bfloat16), 'ctx', scatter_dimensi...]
    all_gather x1 -> x0, waiting for transfers between devices: 66.9 us -> none  [per_device(): whole_kv = lax.all_gather(local_kv, 'ctx', axis=1, tiled=True)]
    unnamed x15 -> x11, local copies, waits for them, and re-layouts: 34.3 us -> 6.75 us
    dynamic_update_slice x48 -> x0, local copies, waits for them, and re-layouts: 21 us -> none  [per_device(): lax.map(partial(attend_block, score_scale=HD ** (-0.5)), (query_rows, gra...]
    scatter-add x1 -> x0, other arithmetic: 19.1 us -> none  [per_device(): placed = jnp.zeros((2, all_blocks, block_len, row_width), jnp.float32).at...]
    another operation x13 -> x0, other arithmetic: 16.7 us -> none
  transfers between devices with their start and end apart: 3 -> 0, of which waited for: 3 -> 0; matrix products, arithmetic and copies ran while one was open for 2% -> 0% of each run, Pallas kernels for 0% -> 0%
where the time goes in v3:
time: 100 us; the launch traced here: 99.9 us
  Pallas kernels  91.7 us (92%)
  local copies, waits for them, and re-layouts  7.54 us (8%)
    pallas_call x1, Pallas kernels, per_device(): pl.pallas_call(step_kernel, out_shape=[wide, wide, home, home], in_specs=...  91.7 us
    unnamed x11, local copies, waits for them, and re-layouts  6.75 us

profile of v3, /device:TPU:1, one launch (start us, length us, event | category | flops | bytes accessed | tf_op | source)
XLA Modules:
  0.0 99.9 jit_solution(4532808248300835430)
XLA Ops:
  0.6 0.8 copy.9
  1.4 0.8 reshape.11.rand
  2.2 91.7 %shard_map.84 = (bf16[1024,1024]{1,0:T(8,128)(2,1)}, bf16[1024,1024]{1,0:T(8,128)(2,1)}, bf16[128,1024]{1,0:T(8,128)(2,1)}, bf16[128,1024]{1,0:T(8,128)(2,1)}) custom-call(s32[384]{0:T(512)} %reshape.11.rand, bf16[1024,1024]{1,0:T(8,128)(2,1)} %q_hbm.1, bf16[1024,1024]{1,0:T(8,128)(2,1)} %g_hbm.1, bf16[128,1024]{1,0:T(8,128)(2,1)} %key_ref.1, ...), custom_call_target="tpu_custom_call" | custom-call | tf_op jit(solution)/shard_map/pallas_call | solution.py:408
  93.9 0.0 copy-start
  93.9 3.2 %copy.14 = bf16[1024,1024]{1,0:T(8,128)(2,1)} copy(bf16[1024,1024]{1,0:T(8,128)(2,1)} %get-tuple-element.8) | data formatting | bytes 4194304
  97.1 0.0 copy-done
  97.1 0.0 copy-start.2
  97.1 0.0 copy-start.1
  97.1 1.3 %copy.15 = bf16[1024,1024]{1,0:T(8,128)(2,1)} copy(bf16[1024,1024]{1,0:T(8,128)(2,1)S(1)} %copy-done) | data formatting | bytes 4194304
  98.4 0.0 copy-done.2
  98.4 0.7 copy.16
  99.1 0.0 copy-done.1
  99.1 0.7 copy.17
Async XLA Ops:
  93.9 3.2 %copy-start = (bf16[1024,1024]{1,0:T(8,128)(2,1)S(1)}, bf16[1024,1024]{1,0:T(8,128)(2,1)}, u32[]{:S(2)}) copy-start(bf16[1024,1024]{1,0:T(8,128)(2,1)} %get-tuple-element.9) | copy-start | bytes 6291460
  97.1 1.3 %copy-start.2 = (bf16[128,1024]{1,0:T(8,128)(2,1)S(1)}, bf16[128,1024]{1,0:T(8,128)(2,1)}, u32[]{:S(2)}) copy-start(bf16[128,1024]{1,0:T(8,128)(2,1)} %get-tuple-element.10) | copy-start | bytes 786436
  97.1 2.0 %copy-start.1 = (bf16[128,1024]{1,0:T(8,128)(2,1)S(1)}, bf16[128,1024]{1,0:T(8,128)(2,1)}, u32[]{:S(2)}) copy-start(bf16[128,1024]{1,0:T(8,128)(2,1)} %get-tuple-element.11) | copy-start | bytes 786436

commit v4 on v3

--- a/solution.py
+++ b/solution.py
@@ -22,16 +22,18 @@
 RECV = QB + 1
 POOL = RECV + CTX * SLOTS
 ENTRIES = 3 + GLOB + RAND
-CHUNK = 512
+CHUNK = 256
 PER = CHUNK // BLK
-HALVES = HEADS // PER
+UNITS = HEADS // PER
+PAIR = 2 * PER
+HALF = 2 * CHUNK
 NAMED = QB * RAND
 EDGE = NAMED + GLOB
 NONE = EDGE + 2
 SUMS = QB + 2 + GLOB
 SCALE = HD**-0.5
 LOG2E = 1.4426950408889634
-MASKED = -1e30
+MASKED = 1e30
 MESH = pl.DeviceIdType.MESH
 ORDER = (
     (0, 1), (1, 0), (0, 3), (3, 0), (1, 1), (2, 0), (3, 3), (0, 2),
@@ -54,7 +56,7 @@
     first = second = jnp.int32(name(None, None))
     count = jnp.int32(0)
     for n in range(NAMED):
-        r = rand[row * NAMED + n]
+        r = rand[n % RAND, row * QB + n // RAND]
         hit = (r >> 3) == owner
         first = jnp.where(hit & (count == 0), name(r, n), first)
         second = jnp.where(hit & (count == 1), name(r, n), second)
@@ -94,14 +96,14 @@
             after = RECV + (me + 1) * SLOTS
             place = jnp.where(near < 0, before, jnp.where(near >= QB, after, near))
             ok = (gid >= GLOB) & (gid < NKB)
-            table[i * ENTRIES + e] = jnp.where(ok, place, 0)
+            table[i * ENTRIES + e] = jnp.where(ok, place, jnp.where(me == 0, 0, RECV))
         for e in range(GLOB):
             table[i * ENTRIES + 3 + e] = jnp.where(me == 0, e, RECV + e)
         for e in range(RAND):
-            owner = rand[me * NAMED + i * RAND + e] >> 3
+            owner = rand[e, me * QB + i] >> 3
             rank = jnp.int32(0)
             for n in range(NAMED):
-                same = ((rand[me * NAMED + n] >> 3) == owner) & (n < i * RAND + e)
+                same = ((rand[n % RAND, me * QB + n // RAND] >> 3) == owner) & (n < i * RAND + e)
                 rank = rank + same.astype(jnp.int32)
             table[i * ENTRIES + 3 + GLOB + e] = RECV + owner * SLOTS + rank
         return carry
@@ -129,11 +131,11 @@
 def step_kernel(
     rand, q_hbm, g_hbm, key_ref, value_ref,
     o_hbm, dq_hbm, dk_ref, dv_ref,
-    q, g, o, dq, probs, inverse, local_k, local_v, pool_k, pool_v, packed_k, packed_v, back_k, back_v,
+    q, g, o, dq, probs, inverse, left, right, out_left, out_right, heads_k, heads_v, local_k, local_v, pool_k, pool_v, packed_k, packed_v, back_k, back_v,
     arrived_k, arrived_v, terms_k, terms_v, sums_k, sums_v, stage_k, stage_v, extra_k, extra_v,
     listed, part, outgoing, returning, places,
     head_send, head_recv, ctx_send, ctx_recv, home_send, home_recv, ret_send, ret_recv,
-    extra_send, extra_recv, own_sem, home_own, in_sem, out_sem,
+    extra_send, extra_recv, own_sem, home_own, in_sem, out_sem, stage_sem,
 ):
     me = lax.axis_index("ctx")
     h = lax.axis_index("kvh")
@@ -148,22 +150,33 @@
     ]
     for copy in loads:
         copy.start()
+    heads_in = (heads_k, heads_v)
+    for t, ref in enumerate((key_ref, value_ref)):
+        for head in range(KVH):
+            loads.append(
+                pltpu.make_async_copy(
+                    ref.at[:, head * HD : (head + 1) * HD], heads_in[t].at[head], stage_sem.at[t, head]
+                )
+            )
+            loads[-1].start()
     greet(me, h)
     cols = lambda head: pl.ds(pl.multiple_of(head * HD, HD), HD)
     heads = lambda: [(dh, lax.rem(h + dh, KVH)) for dh in range(1, KVH)]
     peers = lambda: [ctx_at(me, dz, dx) for dz, dx in ORDER]
     sent = []
     own = []
-    for t, ref in enumerate((key_ref, value_ref)):
+    for t in range(2):
+        for head in range(KVH):
+            loads[2 + t * KVH + head].wait()
         for _, peer in heads():
             sent.append(
                 remote(
-                    ref.at[:, cols(peer)], local[t].at[h],
+                    heads_in[t].at[peer], local[t].at[h],
                     head_send.at[t, peer], head_recv.at[t, h], (me, peer),
                 )
             )
             sent[-1].start()
-        own.append(pltpu.make_async_copy(ref.at[:, cols(h)], local[t].at[h], own_sem.at[t]))
+        own.append(pltpu.make_async_copy(heads_in[t].at[h], local[t].at[h], own_sem.at[t]))
         own[-1].start()
     send_table(rand, me, outgoing)
     for t in range(2):
@@ -198,7 +211,7 @@
             pools[t][b] = local[t][b]
         sums[t][...] = jnp.zeros_like(sums[t])
         terms[t][NONE] = jnp.zeros((HD, BLK), bf)
-    for copy in loads:
+    for copy in loads[:2]:
         copy.wait()
 
     def arrive(t):
@@ -218,9 +231,15 @@
         for e in range(ENTRIES):
             listed[e * BLK : (e + 1) * BLK, :] = pools[t][places[i * ENTRIES + e]]
 
-    def rows_of(i, j):
+    def rows_of(i, first, count):
         rows = pl.ds(pl.multiple_of(i * BLK, BLK), BLK)
-        return [(rows, slice((j * PER + n) * HD, (j * PER + n + 1) * HD)) for n in range(PER)]
+        return [(rows, slice(n * HD, (n + 1) * HD)) for n in range(first, first + count)]
+
+    def unit(i, u):
+        return rows_of(i, u * PER, PER), slice(u * CHUNK, (u + 1) * CHUNK)
+
+    def fold(u, term):
+        part[...] = term if u == 1 else part[...] + term
 
     def stacked(ref, where):
         return jnp.concatenate([ref[w] for w in where], 0)
@@ -267,20 +286,18 @@
             remote(terms[t].at[EDGE], extras[t], extra_send.at[t], extra_recv.at[t], (0, h)).start()
 
     def finish(t, ref):
-        def body(n, carry):
-            peer = lax.rem(me + n, CTX)
+        for dz, dx in ORDER:
+            peer = ctx_at(me, SIDE - dz, SIDE - dx)
             remote(
                 backs[t].at[peer], arrived[t].at[peer],
                 ret_send.at[t, peer], ret_recv.at[t, peer], (peer, h),
             ).wait_recv()
-            for k in range(SLOTS):
-                place = outgoing[peer * 2 + k]
-                term = arrived[t][peer, k].astype(jnp.float32)
-                for b in range(QB):
-                    sums[t][1 + b] += term * (place == b).astype(jnp.float32)
-            return carry
-
-        lax.fori_loop(1, CTX, body, 0)
+            first = arrived[t][peer, 0].astype(jnp.float32)
+            second = arrived[t][peer, 1].astype(jnp.float32)
+            for b in range(QB):
+                sums[t][1 + b] += first * (outgoing[peer * 2] == b).astype(jnp.float32) + second * (
+                    outgoing[peer * 2 + 1] == b
+                ).astype(jnp.float32)
 
         @pl.when(me == 0)
         def _():
@@ -302,54 +319,77 @@
 
     arrive(0)
 
+    def score(i, u, buf):
+        where = rows_of(i, u * PAIR, PAIR)
+        buf[...] = mm(stacked(q, where), listed[...], NT)
+
+    def soften(i, u, buf):
+        where = rows_of(i, u * PAIR, PAIR)
+        span = slice(u * HALF, (u + 1) * HALF)
+        s = buf[...]
+        top = jnp.max(s, 1, keepdims=True) * (SCALE * LOG2E)
+        parts = []
+        for e in range(ENTRIES):
+            gid = me * QB + i - 1 + e
+            ok = (gid >= GLOB) & (gid < NKB)
+            base = top + jnp.where(ok, 0.0, MASKED).astype(jnp.float32) if e < 3 else top
+            parts.append(jnp.exp2(s[:, e * BLK : (e + 1) * BLK] * (SCALE * LOG2E) - base))
+        p = jnp.concatenate(parts, 1)
+        inv = 1.0 / jnp.sum(p, 1, keepdims=True)
+        probs[i, span] = p.astype(bf)
+        inverse[i, span] = inv
+        spread(g, where, stacked(g, where).astype(jnp.float32) * inv)
+
+    def both(ref, i, u):
+        return stacked(ref, rows_of(i, (u - 1) * PER, 2 * PER))
+
     def weigh(i, carry):
-        collect(0, i)
-        for j in range(HALVES):
-            where = rows_of(i, j)
-            s = mm(stacked(q, where), listed[...], NT)
-            parts = []
-            for e in range(ENTRIES):
-                piece = s[:, e * BLK : (e + 1) * BLK]
-                if e < 3:
-                    gid = me * QB + i - 1 + e
-                    ok = (gid >= GLOB) & (gid < NKB)
-                    piece = piece + jnp.where(ok, 0.0, MASKED).astype(jnp.float32)
-                parts.append(piece)
-            s = jnp.concatenate(parts, 1)
-            top = jnp.max(s, 1, keepdims=True)
-            p = jnp.exp2(s * (SCALE * LOG2E) - top * (SCALE * LOG2E))
-            inv = 1.0 / jnp.sum(p, 1, keepdims=True)
-            pb = p.astype(bf)
-            gb = (stacked(g, where).astype(jnp.float32) * inv).astype(bf)
-            probs[i * HALVES + j] = pb
-            inverse[i * HALVES + j] = inv
-            spread(g, where, gb)
-            more = mm(gb, pb, TN)
-            part[...] = more if j == 0 else part[...] + more
+        following = jnp.minimum(i + 1, QB - 1)
+        score(i, 1, right)
+        soften(i, 0, left)
+        collect(0, following)
+        score(following, 0, left)
+        soften(i, 1, right)
+        part[...] = mm(stacked(g, rows_of(i, 0, HEADS)), probs[i], TN)
         bank(1, i, 1.0)
         return carry
 
+    collect(0, 0)
+    score(0, 0, left)
     lax.fori_loop(0, QB, weigh, 0)
     give_back(1)
     arrive(1)
 
+    def project(i, u, buf, out):
+        where, span = unit(i, u)
+        out[...] = mm(probs[i, span], listed[...])
+        buf[:CHUNK] = mm(stacked(g, where), listed[...], NT)
+
+    def grade(i, u, buf, out):
+        where, span = unit(i, u)
+        value = out[...] * inverse[i, span]
+        spread(o, where, value)
+        centre = jnp.sum(stacked(g, where).astype(jnp.float32) * value, 1, keepdims=True)
+        probs[i, span] = (probs[i, span].astype(jnp.float32) * (buf[:CHUNK] - centre)).astype(bf)
+
     def blame(i, carry):
-        collect(1, i)
-        for j in range(HALVES):
-            where = rows_of(i, j)
-            pb = probs[i * HALVES + j]
-            gb = stacked(g, where)
-            out = mm(pb, listed[...]) * inverse[i * HALVES + j]
-            spread(o, where, out)
-            centre = jnp.sum(gb.astype(jnp.float32) * out, 1, keepdims=True)
-            dp = mm(gb, listed[...], NT)
-            ds = (pb.astype(jnp.float32) * (dp - centre)).astype(bf)
-            probs[i * HALVES + j] = ds
-            more = mm(stacked(q, where), ds, TN)
-            part[...] = more if j == 0 else part[...] + more
+        for u in range(UNITS):
+            here, there = (left, right) if u % 2 == 0 else (right, left)
+            out, ahead = (out_left, out_right) if u % 2 == 0 else (out_right, out_left)
+            if u + 1 < UNITS:
+                project(i, u + 1, there, ahead)
+            else:
+                following = jnp.minimum(i + 1, QB - 1)
+                collect(1, following)
+                project(following, 0, there, ahead)
+            grade(i, u, here, out)
+            if u % 2 == 1:
+                fold(u, mm(both(q, i, u), probs[i, (u - 1) * CHUNK : (u + 1) * CHUNK], TN))
         bank(0, i, SCALE)
         return carry
 
+    collect(1, 0)
+    project(0, 0, left, out_left)
     lax.fori_loop(0, QB, blame, 0)
     give_back(0)
     stores = [pltpu.make_async_copy(o, o_hbm, out_sem.at[0])]
@@ -358,8 +398,9 @@
 
     def steer(i, carry):
         collect(0, i)
-        for j in range(HALVES):
-            spread(dq, rows_of(i, j), mm(probs[i * HALVES + j], listed[...]) * SCALE)
+        for u in range(1, UNITS, 2):
+            where = rows_of(i, (u - 1) * PER, 2 * PER)
+            spread(dq, where, mm(probs[i, (u - 1) * CHUNK : (u + 1) * CHUNK], listed[...]) * SCALE)
         return carry
 
     lax.fori_loop(0, QB, steer, 0)
@@ -388,6 +429,33 @@
                 stages[t].at[peer], ref.at[:, cols(peer)],
                 home_send.at[t, peer], home_recv.at[t, peer], (me, peer),
             ).wait_recv()
+
+
+def copy_kernel(*refs):
+    count = len(refs) // 3
+    ins, outs, held = refs[:count], refs[count : 2 * count], refs[2 * count : 3 * count]
+    read_sem, write_sem = refs[3 * count :]
+    steps = []
+    for n in range(count):
+        rows = ins[n].shape[0]
+        size = min(rows, 2 * BLK)
+        for start in range(0, rows, size):
+            steps.append((n, slice(start, start + size)))
+    reads = [
+        pltpu.make_async_copy(ins[n].at[rows], held[n].at[rows], read_sem.at[i])
+        for i, (n, rows) in enumerate(steps)
+    ]
+    writes = [
+        pltpu.make_async_copy(held[n].at[rows], outs[n].at[rows], write_sem.at[i])
+        for i, (n, rows) in enumerate(steps)
+    ]
+    for copy in reads:
+        copy.start()
+    for read, write in zip(reads, writes):
+        read.wait()
+        write.start()
+    for copy in writes:
+        copy.wait()
 
 
 SM = pl.BlockSpec(memory_space=pltpu.SMEM)
@@ -405,16 +473,19 @@
     two = lambda shape, kind: [pltpu.VMEM(shape, kind)] * 2
     wide = jax.ShapeDtypeStruct((tok, HEADS * HD), bf)
     home = jax.ShapeDtypeStruct((BLK, KVH * HD), bf)
-    return pl.pallas_call(
+    results = pl.pallas_call(
         step_kernel,
         out_shape=[wide, wide, home, home],
         in_specs=[SM, ANY, ANY, ANY, ANY],
         out_specs=[ANY] * 4,
         scratch_shapes=[big] * 4
         + [
-            pltpu.VMEM((QB * HALVES, CHUNK, ENTRIES * BLK), bf),
-            pltpu.VMEM((QB * HALVES, CHUNK, 1), f32),
+            pltpu.VMEM((QB, HEADS * BLK, ENTRIES * BLK), bf),
+            pltpu.VMEM((QB, HEADS * BLK, 1), f32),
         ]
+        + two((HALF, ENTRIES * BLK), f32)
+        + two((CHUNK, HD), f32)
+        + two((KVH, BLK, HD), bf)
         + two((QB, BLK, HD), bf)
         + two((POOL, BLK, HD), bf)
         + [slots] * 6
@@ -433,11 +504,20 @@
         + [DMA((2, CTX))] * 2
         + [DMA((2, KVH))] * 2
         + [DMA((2, CTX))] * 2
-        + [DMA((2,))] * 6,
+        + [DMA((2,))] * 6
+        + [DMA((2, KVH))],
         compiler_params=pltpu.CompilerParams(
             collective_id=0, has_side_effects=True, vmem_limit_bytes=VMEM_BYTES
         ),
-    )(random_blocks.reshape(-1), queries, out_grad, keys, values)
+    )(random_blocks.T, queries, out_grad, keys, values)
+    return pl.pallas_call(
+        copy_kernel,
+        out_shape=[wide, wide, home, home],
+        in_specs=[ANY] * 4,
+        out_specs=[ANY] * 4,
+        scratch_shapes=[big] * 2 + two((BLK, KVH * HD), bf) + [DMA((10,))] * 2,
+        compiler_params=pltpu.CompilerParams(vmem_limit_bytes=VMEM_BYTES),
+    )(*results)
 
 
 def solution(mesh):

time: 100 us -> 89.6 us (0.90)
  local copies, waits for them, and re-layouts: 7.54 us -> 0 us
  Pallas kernels: 91.7 us -> 88.9 us
    pallas_call x1, Pallas kernels: 91.7 us -> 84.8 us  [per_device(): pl.pallas_call(step_kernel, out_shape=[wide, wide, home, home], in_specs=...]
    unnamed x11 -> x0, local copies, waits for them, and re-layouts: 6.75 us -> none
    pallas_call x0 -> x1, Pallas kernels: none -> 4.07 us  [per_device(): pl.pallas_call(copy_kernel, out_shape=[wide, wide, home, home], in_specs=...]
where the time goes in v4:
time: 89.6 us; the launch traced here: 89.5 us
  Pallas kernels  88.9 us (99%)
    pallas_call x1, Pallas kernels, per_device(): pl.pallas_call(step_kernel, out_shape=[wide, wide, home, home], in_specs=...  84.8 us
    pallas_call x1, Pallas kernels, per_device(): pl.pallas_call(copy_kernel, out_shape=[wide, wide, home, home], in_specs=...  4.07 us

profile of v4, /device:TPU:1, one launch (start us, length us, event | category | flops | bytes accessed | tf_op | source)
XLA Modules:
  0.0 89.5 jit_solution(4622382281237139993)
XLA Ops:
  0.6 84.8 %shard_map.84 = (bf16[1024,1024]{1,0:T(8,128)(2,1)}, bf16[1024,1024]{1,0:T(8,128)(2,1)}, bf16[128,1024]{1,0:T(8,128)(2,1)}, bf16[128,1024]{1,0:T(8,128)(2,1)}) custom-call(s32[3,128]{1,0:T(4,128)} %bitcast.1, bf16[1024,1024]{1,0:T(8,128)(2,1)} %q_hbm.1, bf16[1024,1024]{1,0:T(8,128)(2,1)} %g_hbm.1, bf16[128,1024]{1,0:T(8,128)(2,1)} %key_ref.1, ...), custom_call_target="tpu_custom_call" | custom-call | tf_op jit(solution)/shard_map/pallas_call | solution.py:476
  85.4 4.1 %shard_map.85 = (bf16[1024,1024]{1,0:T(8,128)(2,1)}, bf16[1024,1024]{1,0:T(8,128)(2,1)}, bf16[128,1024]{1,0:T(8,128)(2,1)}, bf16[128,1024]{1,0:T(8,128)(2,1)}) custom-call(bf16[1024,1024]{1,0:T(8,128)(2,1)} %get-tuple-element.8.refs_0_, bf16[1024,1024]{1,0:T(8,128)(2,1)} %get-tuple-element.9.refs_1_, bf16[128,1024]{1,0:T(8,128)(2,1)} %get-tuple-element.10.refs_2_, ...), custom_call_target="tpu_custom_call" | custom-call | tf_op jit(solution)/shard_map/pallas_call | solution.py:513

commit v5 on v4

--- a/solution.py
+++ b/solution.py
@@ -17,6 +17,7 @@
 HEADS = 8
 SLOTS = 2
 NKB = QB * CTX
+LAG = 4
 SIDE = 4
 EXTRA = QB
 RECV = QB + 1
@@ -130,12 +131,12 @@
 
 def step_kernel(
     rand, q_hbm, g_hbm, key_ref, value_ref,
-    o_hbm, dq_hbm, dk_ref, dv_ref,
-    q, g, o, dq, probs, inverse, left, right, out_left, out_right, heads_k, heads_v, local_k, local_v, pool_k, pool_v, packed_k, packed_v, back_k, back_v,
+    o, dq, dk_ref, dv_ref,
+    q, g, probs, inverse, left, right, out_left, out_right, heads_k, heads_v, local_k, local_v, pool_k, pool_v, packed_k, packed_v, back_k, back_v,
     arrived_k, arrived_v, terms_k, terms_v, sums_k, sums_v, stage_k, stage_v, extra_k, extra_v,
     listed, part, outgoing, returning, places,
     head_send, head_recv, ctx_send, ctx_recv, home_send, home_recv, ret_send, ret_recv,
-    extra_send, extra_recv, own_sem, home_own, in_sem, out_sem, stage_sem,
+    extra_send, extra_recv, own_sem, home_own, in_sem, stage_sem,
 ):
     me = lax.axis_index("ctx")
     h = lax.axis_index("kvh")
@@ -165,6 +166,15 @@
     peers = lambda: [ctx_at(me, dz, dx) for dz, dx in ORDER]
     sent = []
     own = []
+
+    def trail(pack, push):
+        order = peers()
+        for n in range(len(order) + LAG):
+            if n < len(order):
+                pack(order[n])
+            if n >= LAG:
+                push(order[n - LAG])
+
     for t in range(2):
         for head in range(KVH):
             loads[2 + t * KVH + head].wait()
@@ -186,10 +196,12 @@
                 local[t].at[peer], local[t].at[peer],
                 head_send.at[t, peer], head_recv.at[t, peer], (me, peer),
             ).wait_recv()
-        for peer in peers():
+
+        def pack(peer):
             for k in range(SLOTS):
                 packs[t][peer, k] = local[t][outgoing[peer * 2 + k]]
-        for peer in peers():
+
+        def push(peer):
             sent.append(
                 remote(
                     packs[t].at[peer], pools[t].at[pl.ds(RECV + me * SLOTS, SLOTS)],
@@ -197,6 +209,8 @@
                 )
             )
             sent[-1].start()
+
+        trail(pack, push)
 
         @pl.when(me == 0)
         def _():
@@ -269,10 +283,11 @@
             for n in range(GLOB):
                 sums[t][1 + n] += sums[t][QB + 2 + n]
 
-        for peer in peers():
+        def pack(peer):
             for k in range(SLOTS):
                 backs[t][peer, k] = terms[t][returning[peer * 2 + k]]
-        for peer in peers():
+
+        def push(peer):
             sent.append(
                 remote(
                     backs[t].at[peer], arrived[t].at[me],
@@ -280,6 +295,8 @@
                 )
             )
             sent[-1].start()
+
+        trail(pack, push)
 
         @pl.when(me == 1)
         def _():
@@ -392,8 +409,6 @@
     project(0, 0, left, out_left)
     lax.fori_loop(0, QB, blame, 0)
     give_back(0)
-    stores = [pltpu.make_async_copy(o, o_hbm, out_sem.at[0])]
-    stores[-1].start()
     finish(1, dv_ref)
 
     def steer(i, carry):
@@ -404,8 +419,6 @@
         return carry
 
     lax.fori_loop(0, QB, steer, 0)
-    stores.append(pltpu.make_async_copy(dq, dq_hbm, out_sem.at[1]))
-    stores[-1].start()
     finish(0, dk_ref)
     for t in range(2):
 
@@ -421,7 +434,7 @@
 
     for copy in sent:
         copy.wait_send()
-    for copy in own[2:] + stores:
+    for copy in own[2:]:
         copy.wait()
     for t, ref in ((1, dv_ref), (0, dk_ref)):
         for _, peer in heads():
@@ -432,36 +445,22 @@
 
 
 def copy_kernel(*refs):
-    count = len(refs) // 3
-    ins, outs, held = refs[:count], refs[count : 2 * count], refs[2 * count : 3 * count]
-    read_sem, write_sem = refs[3 * count :]
-    steps = []
-    for n in range(count):
-        rows = ins[n].shape[0]
-        size = min(rows, 2 * BLK)
-        for start in range(0, rows, size):
-            steps.append((n, slice(start, start + size)))
-    reads = [
-        pltpu.make_async_copy(ins[n].at[rows], held[n].at[rows], read_sem.at[i])
-        for i, (n, rows) in enumerate(steps)
+    count = len(refs) // 2
+    ins, outs, sem = refs[:count], refs[count : 2 * count], refs[2 * count]
+    writes = [
+        pltpu.make_async_copy(ins[n], outs[n], sem.at[n]) for n in range(count)
     ]
-    writes = [
-        pltpu.make_async_copy(held[n].at[rows], outs[n].at[rows], write_sem.at[i])
-        for i, (n, rows) in enumerate(steps)
-    ]
-    for copy in reads:
+    for copy in writes:
         copy.start()
-    for read, write in zip(reads, writes):
-        read.wait()
-        write.start()
     for copy in writes:
         copy.wait()
 
 
 SM = pl.BlockSpec(memory_space=pltpu.SMEM)
 ANY = pl.BlockSpec(memory_space=pl.ANY)
+VM = pl.BlockSpec(memory_space=pltpu.VMEM)
 DMA = pltpu.SemaphoreType.DMA
-VMEM_BYTES = 60 * 2**20
+VMEM_BYTES = 57 * 2**20
 
 
 def per_device(queries, keys, values, out_grad, random_blocks):
@@ -475,10 +474,10 @@
     home = jax.ShapeDtypeStruct((BLK, KVH * HD), bf)
     results = pl.pallas_call(
         step_kernel,
-        out_shape=[wide, wide, home, home],
+        out_shape=[big, big, pltpu.VMEM((BLK, KVH * HD), bf), pltpu.VMEM((BLK, KVH * HD), bf)],
         in_specs=[SM, ANY, ANY, ANY, ANY],
-        out_specs=[ANY] * 4,
-        scratch_shapes=[big] * 4
+        out_specs=[VM] * 4,
+        scratch_shapes=[big] * 2
         + [
             pltpu.VMEM((QB, HEADS * BLK, ENTRIES * BLK), bf),
             pltpu.VMEM((QB, HEADS * BLK, 1), f32),
@@ -504,7 +503,7 @@
         + [DMA((2, CTX))] * 2
         + [DMA((2, KVH))] * 2
         + [DMA((2, CTX))] * 2
-        + [DMA((2,))] * 6
+        + [DMA((2,))] * 5
         + [DMA((2, KVH))],
         compiler_params=pltpu.CompilerParams(
             collective_id=0, has_side_effects=True, vmem_limit_bytes=VMEM_BYTES
@@ -513,11 +512,11 @@
     return pl.pallas_call(
         copy_kernel,
         out_shape=[wide, wide, home, home],
-        in_specs=[ANY] * 4,
+        in_specs=[VM] * 4,
         out_specs=[ANY] * 4,
-        scratch_shapes=[big] * 2 + two((BLK, KVH * HD), bf) + [DMA((10,))] * 2,
-        compiler_params=pltpu.CompilerParams(vmem_limit_bytes=VMEM_BYTES),
-    )(*results)
+        scratch_shapes=[DMA((4,))],
+        compiler_params=pltpu.CompilerParams(vmem_limit_bytes=2**20),
+    )(*[pltpu.with_memory_space_constraint(x, pltpu.VMEM) for x in results])
 
 
 def solution(mesh):

time: 89.6 us -> 87.6 us (0.978)
  Pallas kernels: 88.9 us -> 86.9 us
    pallas_call x1, Pallas kernels: 4.07 us -> 2.2 us  [per_device(): pl.pallas_call(copy_kernel, out_shape=[wide, wide, home, home], in_specs=...]
where the time goes in v5:
time: 87.6 us; the launch traced here: 87.5 us
  Pallas kernels  86.9 us (99%)
    pallas_call x1, Pallas kernels, per_device(): pl.pallas_call(step_kernel, out_shape=[big, big, pltpu.VMEM((BLK, KVH * H...  84.7 us
    pallas_call x1, Pallas kernels, per_device(): pl.pallas_call(copy_kernel, out_shape=[wide, wide, home, home], in_specs=...  2.2 us

profile of v5, /device:TPU:1, one launch (start us, length us, event | category | flops | bytes accessed | tf_op | source)
XLA Modules:
  0.0 87.5 jit_solution(8242573948197583130)
XLA Ops:
  0.6 84.7 %shard_map.84 = (bf16[1024,1024]{1,0:T(8,128)(2,1)S(1)}, bf16[1024,1024]{1,0:T(8,128)(2,1)S(1)}, bf16[128,1024]{1,0:T(8,128)(2,1)S(1)}, bf16[128,1024]{1,0:T(8,128)(2,1)S(1)}) custom-call(s32[3,128]{1,0:T(4,128)} %bitcast.1, bf16[1024,1024]{1,0:T(8,128)(2,1)} %q_hbm.1, bf16[1024,1024]{1,0:T(8,128)(2,1)} %g_hbm.1, bf16[128,1024]{1,0:T(8,128)(2,1)} %key_ref.1, ...), custom_call_target="tpu_custom_call" | custom-call | tf_op jit(solution)/shard_map/pallas_call | solution.py:475
  85.3 2.2 %shard_map.85 = (bf16[1024,1024]{1,0:T(8,128)(2,1)}, bf16[1024,1024]{1,0:T(8,128)(2,1)}, bf16[128,1024]{1,0:T(8,128)(2,1)}, bf16[128,1024]{1,0:T(8,128)(2,1)}) custom-call(bf16[1024,1024]{1,0:T(8,128)(2,1)S(1)} %get-tuple-element.8.refs_0_, bf16[1024,1024]{1,0:T(8,128)(2,1)S(1)} %get-tuple-element.9.refs_1_, ...), custom_call_target="tpu_custom_call" | custom-call | tf_op jit(solution)/shard_map/pallas_call | solution.py:512

commit v6 on v5

--- a/solution.py
+++ b/solution.py
@@ -114,13 +114,13 @@
 
 def greet(me, h):
     barrier = pltpu.get_barrier_semaphore()
-    for dz, dx in ORDER:
+    for dz, dx in reversed(ORDER):
         peer = (ctx_at(me, dz, dx), h)
         pl.semaphore_signal(barrier, inc=1, device_id=peer, device_id_type=MESH)
     for dh in range(1, KVH):
         peer = (me, lax.rem(h + dh, KVH))
         pl.semaphore_signal(barrier, inc=1, device_id=peer, device_id_type=MESH)
-    pl.semaphore_wait(barrier, CTX + KVH - 2)
+    return lambda: pl.semaphore_wait(barrier, CTX + KVH - 2)
 
 
 def remote(src, dst, send, recv, peer):
@@ -145,6 +145,7 @@
     local = (local_k, local_v)
     arrived, terms, sums = (arrived_k, arrived_v), (terms_k, terms_v), (sums_k, sums_v)
     stages, extras = (stage_k, stage_v), (extra_k, extra_v)
+    met = greet(me, h)
     loads = [
         pltpu.make_async_copy(q_hbm, q, in_sem.at[0]),
         pltpu.make_async_copy(g_hbm, g, in_sem.at[1]),
@@ -160,7 +161,7 @@
                 )
             )
             loads[-1].start()
-    greet(me, h)
+    met()
     cols = lambda head: pl.ds(pl.multiple_of(head * HD, HD), HD)
     heads = lambda: [(dh, lax.rem(h + dh, KVH)) for dh in range(1, KVH)]
     peers = lambda: [ctx_at(me, dz, dx) for dz, dx in ORDER]
@@ -189,7 +190,7 @@
         own.append(pltpu.make_async_copy(heads_in[t].at[h], local[t].at[h], own_sem.at[t]))
         own[-1].start()
     send_table(rand, me, outgoing)
-    for t in range(2):
+    def forward(t):
         own[t].wait()
         for _, peer in heads():
             remote(
@@ -211,6 +212,8 @@
             sent[-1].start()
 
         trail(pack, push)
+        for b in range(QB):
+            pools[t][b] = local[t][b]
 
         @pl.when(me == 0)
         def _():
@@ -218,11 +221,10 @@
                 local[t].at[QB - 1], pools[t].at[EXTRA], extra_send.at[t], extra_recv.at[t], (1, h)
             ).start()
 
+    forward(0)
     place_table(rand, me, places)
     back_table(rand, me, returning)
     for t in range(2):
-        for b in range(QB):
-            pools[t][b] = local[t][b]
         sums[t][...] = jnp.zeros_like(sums[t])
         terms[t][NONE] = jnp.zeros((HD, BLK), bf)
     for copy in loads[:2]:
@@ -335,6 +337,7 @@
         own[-1].start()
 
     arrive(0)
+    forward(1)
 
     def score(i, u, buf):
         where = rows_of(i, u * PAIR, PAIR)

time: 87.6 us -> 86.1 us (0.983)
  Pallas kernels: 86.9 us -> 85.4 us
    pallas_call x1, Pallas kernels: 84.7 us -> 83.2 us  [per_device(): pl.pallas_call(step_kernel, out_shape=[big, big, pltpu.VMEM((BLK, KVH * H...]
where the time goes in v6:
time: 86.1 us; the launch traced here: 86 us
  Pallas kernels  85.4 us (99%)
    pallas_call x1, Pallas kernels, per_device(): pl.pallas_call(step_kernel, out_shape=[big, big, pltpu.VMEM((BLK, KVH * H...  83.2 us
    pallas_call x1, Pallas kernels, per_device(): pl.pallas_call(copy_kernel, out_shape=[wide, wide, home, home], in_specs=...  2.2 us

profile of v6, /device:TPU:1, one launch (start us, length us, event | category | flops | bytes accessed | tf_op | source)
XLA Modules:
  0.0 86.0 jit_solution(904262086750100767)
XLA Ops:
  0.6 83.2 %shard_map.84 = (bf16[1024,1024]{1,0:T(8,128)(2,1)S(1)}, bf16[1024,1024]{1,0:T(8,128)(2,1)S(1)}, bf16[128,1024]{1,0:T(8,128)(2,1)S(1)}, bf16[128,1024]{1,0:T(8,128)(2,1)S(1)}) custom-call(s32[3,128]{1,0:T(4,128)} %bitcast.1, bf16[1024,1024]{1,0:T(8,128)(2,1)} %q_hbm.1, bf16[1024,1024]{1,0:T(8,128)(2,1)} %g_hbm.1, bf16[128,1024]{1,0:T(8,128)(2,1)} %key_ref.1, ...), custom_call_target="tpu_custom_call" | custom-call | tf_op jit(solution)/shard_map/pallas_call | solution.py:478
  83.8 2.2 %shard_map.85 = (bf16[1024,1024]{1,0:T(8,128)(2,1)}, bf16[1024,1024]{1,0:T(8,128)(2,1)}, bf16[128,1024]{1,0:T(8,128)(2,1)}, bf16[128,1024]{1,0:T(8,128)(2,1)}) custom-call(bf16[1024,1024]{1,0:T(8,128)(2,1)S(1)} %get-tuple-element.8.refs_0_, bf16[1024,1024]{1,0:T(8,128)(2,1)S(1)} %get-tuple-element.9.refs_1_, ...), custom_call_target="tpu_custom_call" | custom-call | tf_op jit(solution)/shard_map/pallas_call | solution.py:515

commit v7 on v6

--- a/solution.py
+++ b/solution.py
@@ -176,7 +176,7 @@
             if n >= LAG:
                 push(order[n - LAG])
 
-    for t in range(2):
+    def share(t):
         for head in range(KVH):
             loads[2 + t * KVH + head].wait()
         for _, peer in heads():
@@ -189,6 +189,8 @@
             sent[-1].start()
         own.append(pltpu.make_async_copy(heads_in[t].at[h], local[t].at[h], own_sem.at[t]))
         own[-1].start()
+
+    share(0)
     send_table(rand, me, outgoing)
     def forward(t):
         own[t].wait()
@@ -222,6 +224,7 @@
             ).start()
 
     forward(0)
+    share(1)
     place_table(rand, me, places)
     back_table(rand, me, returning)
     for t in range(2):

time: 86.1 us -> 83.6 us (0.971)
  Pallas kernels: 85.4 us -> 82.8 us
    pallas_call x1, Pallas kernels: 83.2 us -> 80.6 us  [per_device(): pl.pallas_call(step_kernel, out_shape=[big, big, pltpu.VMEM((BLK, KVH * H...]
where the time goes in v7:
time: 83.6 us; the launch traced here: 83.4 us
  Pallas kernels  82.8 us (99%)
    pallas_call x1, Pallas kernels, per_device(): pl.pallas_call(step_kernel, out_shape=[big, big, pltpu.VMEM((BLK, KVH * H...  80.6 us
    pallas_call x1, Pallas kernels, per_device(): pl.pallas_call(copy_kernel, out_shape=[wide, wide, home, home], in_specs=...  2.2 us

profile of v7, /device:TPU:1, one launch (start us, length us, event | category | flops | bytes accessed | tf_op | source)
XLA Modules:
  0.0 83.4 jit_solution(14100295909729424240)
XLA Ops:
  0.6 80.6 %shard_map.84 = (bf16[1024,1024]{1,0:T(8,128)(2,1)S(1)}, bf16[1024,1024]{1,0:T(8,128)(2,1)S(1)}, bf16[128,1024]{1,0:T(8,128)(2,1)S(1)}, bf16[128,1024]{1,0:T(8,128)(2,1)S(1)}) custom-call(s32[3,128]{1,0:T(4,128)} %bitcast.1, bf16[1024,1024]{1,0:T(8,128)(2,1)} %q_hbm.1, bf16[1024,1024]{1,0:T(8,128)(2,1)} %g_hbm.1, bf16[128,1024]{1,0:T(8,128)(2,1)} %key_ref.1, ...), custom_call_target="tpu_custom_call" | custom-call | tf_op jit(solution)/shard_map/pallas_call | solution.py:481
  81.2 2.2 %shard_map.85 = (bf16[1024,1024]{1,0:T(8,128)(2,1)}, bf16[1024,1024]{1,0:T(8,128)(2,1)}, bf16[128,1024]{1,0:T(8,128)(2,1)}, bf16[128,1024]{1,0:T(8,128)(2,1)}) custom-call(bf16[1024,1024]{1,0:T(8,128)(2,1)S(1)} %get-tuple-element.8.refs_0_, bf16[1024,1024]{1,0:T(8,128)(2,1)S(1)} %get-tuple-element.9.refs_1_, ...), custom_call_target="tpu_custom_call" | custom-call | tf_op jit(solution)/shard_map/pallas_call | solution.py:518
